TPU v7x, 512 devices: a whole 4x4x16 slice. The times are simulated.
512 devices in a mesh: space: 16 (over z_hi, x), inst: 32 (over y, z_lo, core).
Axes of the slice: x: 4, y: 4, z: 16 (z_hi: 4, z_lo: 4; z = z_hi * 4 + z_lo), core: 2. Of those that a mesh axis runs over, the one named last changes fastest.
Arguments:
- flow_state: float32 [32, 7, 65536], P('inst', None, 'space'), may hold values from -5.5 to 5.5
- face_nbr: int32 [6, 65536], P(None, 'space'), may hold values from 0 to 5119
- halo_send: int32 [2, 8192], P(None, 'space'), may hold values from 0 to 4095, as said below
- face_area: float32 [3, 6, 65536], P(None, None, 'space'), may hold values from -3 to 3
- cell_volume: float32 [65536], P(('space', 'inst')), may hold values from 0.5 to 2
- flux_left: float32 [7, 7], replicated, may hold values from -2 to 2
- flux_right: float32 [7, 7], replicated, may hold values from -2 to 2
Outputs:
- inverse: float32 [2, 7, 7, 16, 65536], P(None, None, None, None, ('space', 'inst'))
Inputs may be any that keep to these rules, and one draw needn't show every extreme that they name: `halo_send`: within each slab's block of 512 columns, row 0 lists each cell of local indices (7) * 512 to 4095 once and row 1 each cell of local indices 0 to 511 once.
All inputs are finite; a program needn't handle non-finite values.
Results may differ from a plain program's by a relative error of at most 0.0001.
Values sent between devices are 32-bit elements; how exact they have to be, the bound alone decides.
A program may use at most 128 MiB of HBM per device.

v0:
```python
import jax
import jax.numpy as jnp
from jax import lax
from jax.sharding import PartitionSpec as P

INSTANCES = 32
HARM = 16


frequency = 0.1


def shifted(block, axis, distance):
    devices = range(lax.axis_size(axis))
    route = [(i - distance, i) for i in devices if i - distance in devices]
    return lax.ppermute(block, axis, route)


def face_jacobian(face_mean, normal_flux, flux_left, flux_right):
    coupling = flux_left[:, :, None] * flux_right[None, :, :]
    jacobian = jnp.einsum("imj,bmc->bijc", coupling, face_mean, precision=lax.Precision.HIGHEST)
    identity = jnp.eye(face_mean.shape[1], dtype=jnp.float32)
    jacobian = jacobian + normal_flux[:, None, None, :] * identity[None, :, :, None]
    spectral = jnp.max(jnp.sum(jnp.abs(jacobian), axis=2), axis=1) + 0.5
    return (jacobian, spectral, identity)


def face_terms(face_mean, normal_flux, flux_left, flux_right):
    jacobian, spectral, identity = face_jacobian(face_mean, normal_flux, flux_left, flux_right)
    return jnp.sum(
        0.5 * (jacobian + spectral[:, None, None, :] * identity[None, :, :, None]), axis=0
    )


def invert(real_part, imag_part):
    size_vars = real_part.shape[0]
    identity = jnp.broadcast_to(
        jnp.eye(size_vars, dtype=jnp.float32)[:, :, None, None], real_part.shape
    )
    aug_real = jnp.concatenate([real_part, identity], axis=1)
    aug_imag = jnp.concatenate([imag_part, jnp.zeros_like(identity)], axis=1)
    for column in range(size_vars):
        lead_real = aug_real[column, column]
        lead_imag = aug_imag[column, column]
        inverse_norm = 1.0 / (lead_real * lead_real + lead_imag * lead_imag)
        recip_real = lead_real * inverse_norm
        recip_imag = -lead_imag * inverse_norm
        row_real = aug_real[column] * recip_real - aug_imag[column] * recip_imag
        row_imag = aug_real[column] * recip_imag + aug_imag[column] * recip_real
        col_real = aug_real[:, column : column + 1]
        col_imag = aug_imag[:, column : column + 1]
        aug_real = aug_real - (col_real * row_real[None] - col_imag * row_imag[None])
        aug_imag = aug_imag - (col_real * row_imag[None] + col_imag * row_real[None])
        aug_real = aug_real.at[column].set(row_real)
        aug_imag = aug_imag.at[column].set(row_imag)
    return (aug_real[:, size_vars:], aug_imag[:, size_vars:])


def per_device(flow_state, face_nbr, halo_send, face_area, cell_volume, flux_left, flux_right):
    components = flow_state.shape[1]
    cell_count = flow_state.shape[2]
    face_count = face_nbr.shape[0]
    owners = lax.axis_size("inst")
    share_cells = cell_count // owners
    upward = flow_state[:, :, halo_send[0]]
    downward = flow_state[:, :, halo_send[1]]
    from_lower = shifted(upward, "space", 1)
    from_upper = shifted(downward, "space", -1)
    extended = jnp.concatenate([flow_state, from_lower, from_upper], axis=2)
    running = jnp.zeros((components, components, cell_count), jnp.float32)
    for direction in range(face_count):
        neighbour = jnp.take(extended, face_nbr[direction], axis=2)
        face_mean = 0.5 * (flow_state + neighbour)
        normals = face_area[:, direction]
        normal_flux = (
            face_mean[:, 1] * normals[0]
            + face_mean[:, 2] * normals[1]
            + face_mean[:, 3] * normals[2]
        )
        face_mean, normal_flux = (face_mean, normal_flux)
        running = running + face_terms(face_mean, normal_flux, flux_left, flux_right)
    everything = lax.psum(running, "inst")
    summed = lax.dynamic_slice_in_dim(
        everything, lax.axis_index("inst") * share_cells, share_cells, 2
    )
    jacobian_mean = summed / (face_count * INSTANCES)
    harmonics = jnp.arange(1, HARM + 1, dtype=jnp.int32).astype(jnp.float32)
    imag_shift = harmonics[:, None] * frequency * cell_volume[None, :]
    real_part = jnp.broadcast_to(
        jacobian_mean[:, :, None, :], (components, components, HARM, share_cells)
    )
    imag_part = jnp.eye(components, dtype=jnp.float32)[:, :, None, None] * imag_shift[None, None]
    inv_real, inv_imag = invert(real_part, imag_part)
    return jnp.stack([inv_real, inv_imag])


def solution(mesh):
    placed = (
        P("inst", None, "space"),
        P(None, "space"),
        P(None, "space"),
        P(None, None, "space"),
        P(("space", "inst")),
        P(),
        P(),
    )
    return jax.shard_map(
        per_device,
        mesh=mesh,
        in_specs=placed,
        out_specs=P(None, None, None, None, ("space", "inst")),
        check_vma=False,
    )
```

profile of v0, /device:TPU:7, one launch (start us, length us, event | category | flops | bytes accessed | tf_op | source)
XLA Modules:
  0.0 461.6 jit_solution(6853187282242230879)
XLA Ops:
  6.5 1.6 copy.196
  8.2 1.0 gather_fusion
  9.2 8.7 %collective-permute-start = (f32[1,7,512]{1,2,0:T(8,128)S(1)}, f32[1,7,512]{1,2,0:T(8,128)S(1)}, u32[]{:S(2)}, u32[]{:S(2)}) collective-permute-start(f32[1,7,512]{1,2,0:T(8,128)S(1)} %bitcast.360), channel_id=1, source_target_pairs={{0,32},{32,64},{64,96},{96,128},{128,160},{160,192},{192,224},{224... | collective-permute-start | bytes 43016 | tf_op jit(solution)/shard_map/ppermute | solution.py:16
  18.0 1.0 gather_fusion.1
  19.0 1.9 collective-permute-start.1
  21.0 0.1 fusion.97
  21.1 0.6 compare_and_fusion
  21.7 0.6 compare_and_fusion.2
  22.3 0.6 compare_and_fusion.4
  22.9 0.1 copy.199
  23.0 27.6 %collective-permute-done.1 = f32[1,7,512]{1,2,0:T(8,128)S(1)} collective-permute-done((f32[1,7,512]{1,2,0:T(8,128)S(1)}, f32[1,7,512]{1,2,0:T(8,128)S(1)}, u32[]{:S(2)}, u32[]{:S(2)}) %collective-permute-start.1) | collective-permute-done | bytes 14368 | tf_op jit(solution)/shard_map/ppermute | solution.py:16
  50.7 1.8 maximum_bitcast_fusion
  52.4 14.2 %gather_fusion.2 = f32[4096,7]{1,0:T(8,128)} fusion(f32[7,5120]{0,1:T(8,128)S(1)} %maximum_bitcast_fusion, s32[4096]{0:T(1024)S(1)} %fusion.74), kind=kCustom, calls=%fused_computation.clone | custom fusion | bytes 245760 | tf_op jit(solution)/shard_map/jit(_take)/gather | solution.py:72
  66.6 2.2 copy.197
  68.8 14.2 %gather_fusion.3 = f32[4096,7]{1,0:T(8,128)} fusion(f32[7,5120]{0,1:T(8,128)S(1)} %maximum_bitcast_fusion, s32[4096]{0:T(1024)S(1)} %fusion.75), kind=kCustom, calls=%fused_computation.1.clone | custom fusion | bytes 245760 | tf_op jit(solution)/shard_map/jit(_take)/gather | solution.py:72
  83.0 2.2 copy.200
  85.2 14.2 %gather_fusion.4 = f32[4096,7]{1,0:T(8,128)} fusion(f32[7,5120]{0,1:T(8,128)S(1)} %maximum_bitcast_fusion, s32[4096]{0:T(1024)S(1)} %fusion.76), kind=kCustom, calls=%fused_computation.2.clone | custom fusion | bytes 245760 | tf_op jit(solution)/shard_map/jit(_take)/gather | solution.py:72
  99.4 2.2 copy.202
  101.6 14.2 %gather_fusion.5 = f32[4096,7]{1,0:T(8,128)} fusion(f32[7,5120]{0,1:T(8,128)S(1)} %maximum_bitcast_fusion, s32[4096]{0:T(1024)S(1)} %fusion.77), kind=kCustom, calls=%fused_computation.3.clone | custom fusion | bytes 245760 | tf_op jit(solution)/shard_map/jit(_take)/gather | solution.py:72
  115.8 2.9 copy.204
  118.6 14.2 %gather_fusion.6 = f32[4096,7]{1,0:T(8,128)} fusion(f32[7,5120]{0,1:T(8,128)S(1)} %maximum_bitcast_fusion, s32[4096]{0:T(1024)S(1)} %fusion.78), kind=kCustom, calls=%fused_computation.4.clone | custom fusion | bytes 245760 | tf_op jit(solution)/shard_map/jit(_take)/gather | solution.py:72
  132.8 2.9 copy.206
  135.7 14.2 %gather_fusion.7 = f32[4096,7]{1,0:T(8,128)} fusion(f32[7,5120]{0,1:T(8,128)S(1)} %maximum_bitcast_fusion, s32[4096]{0:T(1024)S(1)} %fusion.79), kind=kCustom, calls=%fused_computation.5.clone | custom fusion | bytes 245760 | tf_op jit(solution)/shard_map/jit(_take)/gather | solution.py:72
  149.9 2.3 copy.208
  152.3 0.2 fusion.7
  152.5 1.6 fusion.36
  154.1 1.1 abs_reduce_fusion.5
  155.3 1.1 abs_reduce_fusion.4
  156.5 1.1 abs_reduce_fusion.3
  157.7 1.6 fusion.30
  159.4 2.0 abs_reduce_fusion.2
  161.5 2.1 abs_reduce_fusion.1
  163.6 2.1 abs_reduce_fusion
  165.8 3.3 multiply_bitcast_fusion
  169.1 0.0 all-reduce.3.cloned.1.call-update
  169.1 0.1 broadcast_multiply_fusion.1
  169.2 0.1 broadcast_multiply_fusion
  169.3 281.1 %all-reduce.3.cloned.1.call-done = f32[7,7,4096]{2,1,0:T(8,128)} async-done(((f32[7,7,4096]{2,1,0:T(8,128)}), f32[7,7,4096]{2,1,0:T(8,128)}) %all-reduce.3.cloned.1.call-update) | async-done | bytes 802832 | tf_op jit(solution)/shard_map/psum | solution.py:82
  450.4 0.8 dynamic-slice_multiply_fusion
  451.2 0.1 broadcast_in_dim.22
  451.4 0.2 fusion.6
  451.7 0.2 subtract_subtract_fusion.5
  452.1 0.2 subtract_subtract_fusion.4
  452.4 0.2 subtract_subtract_fusion.3
  452.8 0.2 subtract_subtract_fusion.2
  453.1 0.2 subtract_subtract_fusion.1
  453.5 0.2 subtract_subtract_fusion
  453.8 1.0 pad_maximum_fusion.1
  (94 shorter events, 1.1 us)
Async XLA Ops:
  6.5 1.6 copy-start.11
  6.5 14.4 %copy-start.5 = (s32[6,4096]{1,0:T(8,128)S(1)}, s32[6,4096]{1,0:T(8,128)}, u32[]{:S(2)}) copy-start(s32[6,4096]{1,0:T(8,128)} %param.38) | copy-start | bytes 294916
  6.5 16.4 %copy-start.12 = (f32[7,7]{1,0:T(8,128)S(1)}, f32[7,7]{1,0:T(8,128)}, u32[]{:S(2)}) copy-start(f32[7,7]{1,0:T(8,128)} %param.43) | copy-start | bytes 592
  6.5 443.9 %all-reduce.3.cloned.1.call-start = ((), (), s32[]{:S(2)}) async-start(), calls=%async_computation | async-start | bytes 1835008 | tf_op jit(solution)/shard_map/psum | solution.py:82
  8.1 14.9 %copy-start = (f32[1,7,4096]{1,2,0:T(8,128)}, f32[1,7,4096]{1,2,0:T(8,128)S(1)}, u32[]{:S(2)}) copy-start(f32[1,7,4096]{1,2,0:T(8,128)S(1)} %copy.196) | copy-start | bytes 344068
  9.2 13.8 %collective-permute-start = (f32[1,7,512]{1,2,0:T(8,128)S(1)}, f32[1,7,512]{1,2,0:T(8,128)S(1)}, u32[]{:S(2)}, u32[]{:S(2)}) collective-permute-start(f32[1,7,512]{1,2,0:T(8,128)S(1)} %bitcast.360), channel_id=1, source_target_pairs={{0,32},{32,64},{64,96},{96,128},{128,160},{160,192},{192,224},{224... | collective-permute-start | bytes 43016 | tf_op jit(solution)/shard_map/ppermute | solution.py:16
  19.0 31.6 %collective-permute-start.1 = (f32[1,7,512]{1,2,0:T(8,128)S(1)}, f32[1,7,512]{1,2,0:T(8,128)S(1)}, u32[]{:S(2)}, u32[]{:S(2)}) collective-permute-start(f32[1,7,512]{1,2,0:T(8,128)S(1)} %bitcast.361), channel_id=1, source_target_pairs={{32,0},{64,32},{96,64},{128,96},{160,128},{192,160},{224,192},{256... | collective-permute-start | bytes 43016 | tf_op jit(solution)/shard_map/ppermute | solution.py:16
  149.8 2.4 copy-start.1
  149.8 2.4 copy-start.2
  149.8 2.4 copy-start.3
  149.8 2.4 copy-start.6
  149.8 2.4 copy-start.7
  149.9 2.4 copy-start.8
  149.9 2.4 copy-start.9
  149.9 2.4 copy-start.10
  149.9 4.2 copy-start.4
  165.8 3.3 copy-start.13
Sparse Core Ops, SparseCore 0:
  169.2 281.1 all-reduce.2
where the time goes:
time: 464 us; the launch traced here: 462 us
  waiting for transfers between devices  309 us (67%)
  local copies, waits for them, and re-layouts  104 us (22%)
  other arithmetic  14.7 us (3%)
  between operations  14.1 us (3%)
  starting transfers between devices  10.7 us (2%)
  matrix products  9.63 us (2%)
    psum x1, waiting for transfers between devices, per_device(): everything = lax.psum(running, 'inst')  281 us
    gather x12, local copies, waits for them, and re-layouts, per_device(): neighbour = jnp.take(extended, face_nbr[direction], axis=2)  99.7 us
    ppermute x2, waiting for transfers between devices, shifted(): return lax.ppermute(block, axis, route)  27.6 us
    ppermute x2, starting transfers between devices, shifted(): return lax.ppermute(block, axis, route)  10.7 us
    dot_general x6, matrix products, face_jacobian(): jnp.einsum('imj,bmc->bijc', coupling, face_mean, precision=lax.Precision....  9.63 us
  transfers between devices with their start and end apart: 3, of which 2 were waited for; matrix products, arithmetic and copies ran while one was open for 1% of the time, Pallas kernels for 0%

commit v1 on v0

v1 whole, which is shorter than its diff:
```python
import functools

import jax
import jax.numpy as jnp
from jax import lax
from jax.experimental import pallas as pl
from jax.experimental.pallas import tpu as pltpu
from jax.sharding import PartitionSpec as P

INSTANCES = 32
HARM = 16
NVAR = 7
FACES = 6
LANES = 128

frequency = 0.1


def lane_gather(rows, lane):
    return jnp.take_along_axis(rows, lane, axis=1, mode="promise_in_bounds")


def wide(row):
    return jnp.broadcast_to(row, (8, LANES))


def sums_kernel(
    slabs, owners,
    state, nbr, send, area, left, right,
    out,
    idx, areas, halo_idx, up, down, from_low, from_high, nb, coupling, outbox, inbox,
    halo_send_sem, halo_recv_sem, send_sem, recv_sem,
):
    space = lax.axis_index("space")
    inst = lax.axis_index("inst")
    above = lax.rem(space + 1, slabs)
    below = lax.rem(space + slabs - 1, slabs)

    barrier = pltpu.get_barrier_semaphore()
    pl.semaphore_signal(barrier, inc=1, device_id={"space": above}, device_id_type=pl.DeviceIdType.MESH)
    pl.semaphore_signal(barrier, inc=1, device_id={"space": below}, device_id_type=pl.DeviceIdType.MESH)

    def greet(step, carry):
        other = lax.rem(inst + step, owners)
        pl.semaphore_signal(barrier, inc=1, device_id={"inst": other}, device_id_type=pl.DeviceIdType.MESH)
        return carry

    lax.fori_loop(1, owners, greet, 0)

    for k in range(4):
        halo_idx[pl.ds(k, 1)] = send[0:1, LANES * k : LANES * (k + 1)]
        halo_idx[pl.ds(4 + k, 1)] = send[1:2, LANES * k : LANES * (k + 1)]
    hidx = halo_idx[...]
    hlane = hidx & (LANES - 1)
    hrow = (hidx >> 7) & 3
    upper = lax.broadcasted_iota(jnp.int32, (8, LANES), 0) < 4
    for c in range(NVAR):
        found = jnp.zeros((8, LANES), jnp.float32)
        for q in range(4):
            rows = jnp.where(upper, wide(state[c, pl.ds(28 + q, 1)]), wide(state[c, pl.ds(q, 1)]))
            found = jnp.where(hrow == q, lane_gather(rows, hlane), found)
        up[pl.ds(4 * c, 4)] = found[0:4]
        down[pl.ds(4 * c, 4)] = found[4:8]

    def regroup(k, carry):
        q = k // 8
        s = lax.rem(k, 8)
        col = pl.multiple_of(k * LANES, LANES)
        idx[pl.ds(q * 48 + s, FACES, stride=8)] = nbr[:, pl.ds(col, LANES)]
        for x in range(3):
            areas[x, pl.ds(q * 48 + s, FACES, stride=8)] = area[x, :, pl.ds(col, LANES)]
        return carry

    lax.fori_loop(0, 32, regroup, 0)

    for i in range(NVAR):
        for m in range(NVAR):
            for j in range(NVAR):
                coupling[(i * NVAR + m) * NVAR + j] = jnp.full((8, LANES), left[i, m] * right[m, j], jnp.float32)

    pl.semaphore_wait(barrier, owners + 1)
    rise = pltpu.make_async_remote_copy(
        src_ref=up, dst_ref=from_low, send_sem=halo_send_sem.at[0], recv_sem=halo_recv_sem.at[0],
        device_id={"space": above}, device_id_type=pl.DeviceIdType.MESH,
    )
    sink = pltpu.make_async_remote_copy(
        src_ref=down, dst_ref=from_high, send_sem=halo_send_sem.at[1], recv_sem=halo_recv_sem.at[1],
        device_id={"space": below}, device_id_type=pl.DeviceIdType.MESH,
    )
    rise.start()
    sink.start()

    def local(g, carry):
        cells = idx[pl.ds(pl.multiple_of(g * 8, 8), 8)]
        lane = cells & (LANES - 1)
        row = cells >> 7
        found = [jnp.zeros((8, LANES), jnp.float32) for _ in range(NVAR)]
        for r in range(32):
            here = row == r
            for c in range(NVAR):
                found[c] = jnp.where(here, lane_gather(wide(state[c, pl.ds(r, 1)]), lane), found[c])
        for c in range(NVAR):
            nb[g, c] = found[c]
        return carry

    lax.fori_loop(0, 4 * FACES, local, 0)

    rise.wait()
    sink.wait()
    from_low[...] = jnp.where(space > 0, from_low[...], 0.0)
    from_high[...] = jnp.where(space < slabs - 1, from_high[...], 0.0)

    def group(q, carry):
        first = pl.multiple_of(q * 8, 8)

        def face(d, totals):
            g = q * FACES + d
            at = pl.multiple_of(g * 8, 8)
            cells = idx[pl.ds(at, 8)]
            lane = cells & (LANES - 1)
            row = cells >> 7
            found = [nb[g, c] for c in range(NVAR)]
            for r in range(8):
                here = row == 32 + r
                source = from_low if r < 4 else from_high
                for c in range(NVAR):
                    line = source[pl.ds(4 * c + r % 4, 1)]
                    found[c] = jnp.where(here, lane_gather(wide(line), lane), found[c])
            mean = [0.5 * (state[c, pl.ds(first, 8)] + found[c]) for c in range(NVAR)]
            flux = (
                mean[1] * areas[0, pl.ds(at, 8)]
                + mean[2] * areas[1, pl.ds(at, 8)]
                + mean[3] * areas[2, pl.ds(at, 8)]
            )
            largest = None
            for i in range(NVAR):
                row_sum = None
                for j in range(NVAR):
                    entry = flux if i == j else None
                    for m in range(NVAR):
                        term = coupling[(i * NVAR + m) * NVAR + j] * mean[m]
                        entry = term if entry is None else entry + term
                    entry = jnp.abs(entry)
                    row_sum = entry if row_sum is None else row_sum + entry
                largest = row_sum if largest is None else jnp.maximum(largest, row_sum)
            last = flux + (largest + 0.5)
            return tuple(t + x for t, x in zip(totals, mean + [last]))

        totals = lax.fori_loop(0, FACES, face, tuple(jnp.zeros((8, LANES), jnp.float32) for _ in range(8)))
        for c in range(8):
            outbox[pl.ds(q * 64 + c, 8, stride=8)] = totals[c]

        def post(k, carry):
            owner = q * 8 + k

            @pl.when(owner != inst)
            def _():
                slot = lax.rem(inst - owner + owners, owners) - 1
                pltpu.make_async_remote_copy(
                    src_ref=outbox.at[pl.ds(pl.multiple_of(owner * 8, 8), 8)],
                    dst_ref=inbox.at[pl.ds(pl.multiple_of(slot * 8, 8), 8)],
                    send_sem=send_sem, recv_sem=recv_sem,
                    device_id={"inst": owner}, device_id_type=pl.DeviceIdType.MESH,
                ).start()

            return carry

        lax.fori_loop(0, 8, post, 0)
        return carry

    lax.fori_loop(0, 4, group, 0)
    pltpu.make_async_copy(inbox, inbox, recv_sem).wait()
    total = outbox[pl.ds(pl.multiple_of(inst * 8, 8), 8)]
    for k in range(31):
        total = total + inbox[8 * k : 8 * k + 8]
    out[...] = total
    pltpu.make_async_copy(inbox, inbox, send_sem).wait()


def invert_kernel(sums, volume, left, right, out):
    scale = 1.0 / (2.0 * FACES * INSTANCES)
    part = [jnp.broadcast_to(sums[pl.ds(m, 1)], (8, LANES)) for m in range(NVAR + 1)]
    harmonic = lax.broadcasted_iota(jnp.int32, (HARM, LANES), 0).astype(jnp.float32) + 1.0
    shift = harmonic * frequency * jnp.broadcast_to(volume[...], (HARM, LANES))
    real = {}
    imag = {}
    for i in range(NVAR):
        for j in range(NVAR):
            entry = part[NVAR] if i == j else None
            for m in range(NVAR):
                term = (left[i, m] * right[m, j]) * part[m]
                entry = term if entry is None else entry + term
            entry = entry * scale
            real[i, j] = jnp.concatenate([entry, entry], axis=0)
            imag[i, j] = shift if i == j else None

    def product(ar, ai, br, bi):
        if ai is None and bi is None:
            return ar * br, None
        if ai is None:
            return ar * br, ar * bi
        if bi is None:
            return ar * br, ai * br
        return ar * br - ai * bi, ar * bi + ai * br

    for k in range(NVAR):
        pr, pi = real[k, k], imag[k, k]
        norm = 1.0 / (pr * pr + pi * pi)
        pr, pi = pr * norm, -pi * norm
        for j in range(NVAR):
            if j != k:
                real[k, j], imag[k, j] = product(real[k, j], imag[k, j], pr, pi)
        real[k, k], imag[k, k] = pr, pi
        for i in range(NVAR):
            if i == k:
                continue
            fr, fi = real[i, k], imag[i, k]
            for j in range(NVAR):
                if j == k:
                    continue
                xr, xi = product(fr, fi, real[k, j], imag[k, j])
                real[i, j] = real[i, j] - xr
                if xi is not None:
                    imag[i, j] = -xi if imag[i, j] is None else imag[i, j] - xi
            xr, xi = product(fr, fi, pr, pi)
            real[i, k], imag[i, k] = -xr, -xi
    for i in range(NVAR):
        for j in range(NVAR):
            out[0, i, j] = real[i, j]
            out[1, i, j] = imag[i, j]


def per_device(flow_state, face_nbr, halo_send, face_area, cell_volume, flux_left, flux_right):
    slabs = lax.axis_size("space")
    owners = lax.axis_size("inst")
    share = cell_volume.shape[0]
    state = flow_state.reshape(NVAR, 32, LANES)
    vmem = pl.BlockSpec(memory_space=pltpu.VMEM)
    smem = pl.BlockSpec(memory_space=pltpu.SMEM)
    f32 = jnp.float32
    sums = pl.pallas_call(
        functools.partial(sums_kernel, slabs, owners),
        out_shape=jax.ShapeDtypeStruct((8, LANES), f32),
        in_specs=[vmem, vmem, vmem, vmem, smem, smem],
        out_specs=vmem,
        scratch_shapes=[
            pltpu.VMEM((192, LANES), jnp.int32),
            pltpu.VMEM((3, 192, LANES), f32),
            pltpu.VMEM((8, LANES), jnp.int32),
            pltpu.VMEM((28, LANES), f32),
            pltpu.VMEM((28, LANES), f32),
            pltpu.VMEM((28, LANES), f32),
            pltpu.VMEM((28, LANES), f32),
            pltpu.VMEM((24, NVAR, 8, LANES), f32),
            pltpu.VMEM((343, 8, LANES), f32),
            pltpu.VMEM((256, LANES), f32),
            pltpu.VMEM((248, LANES), f32),
            pltpu.SemaphoreType.DMA((2,)),
            pltpu.SemaphoreType.DMA((2,)),
            pltpu.SemaphoreType.DMA,
            pltpu.SemaphoreType.DMA,
        ],
        compiler_params=pltpu.CompilerParams(collective_id=0, has_side_effects=True),
        name="sums",
    )(state, face_nbr, halo_send, face_area, flux_left, flux_right)
    return pl.pallas_call(
        invert_kernel,
        out_shape=jax.ShapeDtypeStruct((2, NVAR, NVAR, HARM, share), f32),
        in_specs=[vmem, vmem, smem, smem],
        out_specs=vmem,
        name="invert",
    )(sums, cell_volume.reshape(1, share), flux_left, flux_right)


def solution(mesh):
    placed = (
        P("inst", None, "space"),
        P(None, "space"),
        P(None, "space"),
        P(None, None, "space"),
        P(("space", "inst")),
        P(),
        P(),
    )
    return jax.shard_map(
        per_device,
        mesh=mesh,
        in_specs=placed,
        out_specs=P(None, None, None, None, ("space", "inst")),
        check_vma=False,
    )
```

time: 464 us -> 37.1 us (0.08)
  the two profiles are of different devices: /device:TPU:7 before, /device:TPU:25 now
where the time goes in v1:
time: 37.1 us; the launch traced here: 36.9 us
  Pallas kernels  36.9 us (99%)
    pallas_call x1, Pallas kernels, per_device(): pl.pallas_call(functools.partial(sums_kernel, slabs, owners), out_shape=j...  34.2 us
    pallas_call x1, Pallas kernels, per_device(): pl.pallas_call(invert_kernel, out_shape=jax.ShapeDtypeStruct((2, NVAR, NV...  2.69 us

profile of v1, /device:TPU:25, one launch (start us, length us, event | category | flops | bytes accessed | tf_op | source)
XLA Modules:
  0.0 36.9 jit_solution(7465082182546386940)
XLA Ops:
  0.0 34.2 %sums.1 = f32[8,128]{1,0:T(8,128)} custom-call(f32[7,32,128]{2,1,0:T(8,128)} %bitcast.2, s32[6,4096]{1,0:T(8,128)} %nbr.1, s32[2,512]{1,0:T(2,128)} %send.1, f32[3,6,4096]{2,1,0:T(8,128)} %area.1, f32[7,7]{1,0:T(8,128)} %left.3, f32[7,7]{1,0:T(8,128)} %right.3), custom_call_target="tpu_custom_call" | custom-call | tf_op jit(solution)/shard_map/sums/pallas_call | solution.py:241
  34.2 2.7 %invert.1 = f32[2,7,7,16,128]{4,3,2,1,0:T(8,128)} custom-call(f32[8,128]{1,0:T(8,128)} %sums.1, f32[1,128]{1,0:T(1,128)} %bitcast.3, f32[7,7]{1,0:T(8,128)} %left.3, f32[7,7]{1,0:T(8,128)} %right.3), custom_call_target="tpu_custom_call" | custom-call | tf_op jit(solution)/shard_map/invert/pallas_call | solution.py:266

commit v2 on v1

--- a/solution.py
+++ b/solution.py
@@ -24,17 +24,42 @@
     return jnp.broadcast_to(row, (8, LANES))
 
 
+def bits_select(rows, index, bits):
+    for b in range(bits):
+        odd = ((index >> b) & 1) == 1
+        rows = [jnp.where(odd, rows[k + 1], rows[k]) for k in range(0, len(rows), 2)]
+    return rows[0]
+
+
+def two_parts(value):
+    high = value.astype(jnp.bfloat16).astype(jnp.float32)
+    return high, (value - high).astype(jnp.bfloat16).astype(jnp.float32)
+
+
 def sums_kernel(
     slabs, owners,
+    state_hbm, nbr_hbm, send_hbm, area_hbm, left_hbm, right_hbm,
+    out,
     state, nbr, send, area, left, right,
-    out,
-    idx, areas, halo_idx, up, down, from_low, from_high, nb, coupling, outbox, inbox,
-    halo_send_sem, halo_recv_sem, send_sem, recv_sem,
+    idx, areas, halo_idx, up, down, from_low, from_high, table_rows, table, factors, weights,
+    near, work, outbox, inbox,
+    in_sem, halo_send_sem, halo_recv_sem, send_sem, recv_sem,
 ):
     space = lax.axis_index("space")
     inst = lax.axis_index("inst")
     above = lax.rem(space + 1, slabs)
     below = lax.rem(space + slabs - 1, slabs)
+    f32 = jnp.float32
+    bf16 = jnp.bfloat16
+
+    loads = [
+        pltpu.make_async_copy(src, dst, in_sem.at[k])
+        for k, (src, dst) in enumerate(
+            [(state_hbm, state), (send_hbm, send), (nbr_hbm, nbr), (left_hbm, left), (right_hbm, right), (area_hbm, area)]
+        )
+    ]
+    for load in loads:
+        load.start()
 
     barrier = pltpu.get_barrier_semaphore()
     pl.semaphore_signal(barrier, inc=1, device_id={"space": above}, device_id_type=pl.DeviceIdType.MESH)
@@ -47,6 +72,8 @@
 
     lax.fori_loop(1, owners, greet, 0)
 
+    loads[0].wait()
+    loads[1].wait()
     for k in range(4):
         halo_idx[pl.ds(k, 1)] = send[0:1, LANES * k : LANES * (k + 1)]
         halo_idx[pl.ds(4 + k, 1)] = send[1:2, LANES * k : LANES * (k + 1)]
@@ -55,55 +82,111 @@
     hrow = (hidx >> 7) & 3
     upper = lax.broadcasted_iota(jnp.int32, (8, LANES), 0) < 4
     for c in range(NVAR):
-        found = jnp.zeros((8, LANES), jnp.float32)
+        found = jnp.zeros((8, LANES), f32)
         for q in range(4):
             rows = jnp.where(upper, wide(state[c, pl.ds(28 + q, 1)]), wide(state[c, pl.ds(q, 1)]))
             found = jnp.where(hrow == q, lane_gather(rows, hlane), found)
         up[pl.ds(4 * c, 4)] = found[0:4]
         down[pl.ds(4 * c, 4)] = found[4:8]
 
+    pl.semaphore_wait(barrier, owners + 1)
+    rise = pltpu.make_async_remote_copy(
+        src_ref=up, dst_ref=from_low, send_sem=halo_send_sem.at[0], recv_sem=halo_recv_sem.at[0],
+        device_id={"space": above}, device_id_type=pl.DeviceIdType.MESH,
+    )
+    sink = pltpu.make_async_remote_copy(
+        src_ref=down, dst_ref=from_high, send_sem=halo_send_sem.at[1], recv_sem=halo_recv_sem.at[1],
+        device_id={"space": below}, device_id_type=pl.DeviceIdType.MESH,
+    )
+    rise.start()
+    sink.start()
+
+    for c in range(NVAR):
+        table_rows[pl.ds(c, 32, stride=8)] = state[c]
+    table_rows[pl.ds(NVAR, 32, stride=8)] = jnp.zeros((32, LANES), f32)
+    high, rest = two_parts(table_rows[...])
+    table[:, 0:LANES] = high.astype(bf16)
+    table[:, LANES : 2 * LANES] = rest.astype(bf16)
+
+    loads[2].wait()
+
     def regroup(k, carry):
         q = k // 8
         s = lax.rem(k, 8)
         col = pl.multiple_of(k * LANES, LANES)
         idx[pl.ds(q * 48 + s, FACES, stride=8)] = nbr[:, pl.ds(col, LANES)]
-        for x in range(3):
-            areas[x, pl.ds(q * 48 + s, FACES, stride=8)] = area[x, :, pl.ds(col, LANES)]
-        return carry
-
-    lax.fori_loop(0, 32, regroup, 0)
-
-    for i in range(NVAR):
-        for m in range(NVAR):
-            for j in range(NVAR):
-                coupling[(i * NVAR + m) * NVAR + j] = jnp.full((8, LANES), left[i, m] * right[m, j], jnp.float32)
-
-    pl.semaphore_wait(barrier, owners + 1)
-    rise = pltpu.make_async_remote_copy(
-        src_ref=up, dst_ref=from_low, send_sem=halo_send_sem.at[0], recv_sem=halo_recv_sem.at[0],
-        device_id={"space": above}, device_id_type=pl.DeviceIdType.MESH,
-    )
-    sink = pltpu.make_async_remote_copy(
-        src_ref=down, dst_ref=from_high, send_sem=halo_send_sem.at[1], recv_sem=halo_recv_sem.at[1],
-        device_id={"space": below}, device_id_type=pl.DeviceIdType.MESH,
-    )
-    rise.start()
-    sink.start()
-
-    def local(g, carry):
+        return carry
+
+    lax.fori_loop(0, 32, regroup, 0, unroll=8)
+
+    def by_lanes(g):
         cells = idx[pl.ds(pl.multiple_of(g * 8, 8), 8)]
         lane = cells & (LANES - 1)
         row = cells >> 7
-        found = [jnp.zeros((8, LANES), jnp.float32) for _ in range(NVAR)]
+        found = [jnp.zeros((8, LANES), f32) for _ in range(NVAR)]
         for r in range(32):
             here = row == r
             for c in range(NVAR):
                 found[c] = jnp.where(here, lane_gather(wide(state[c, pl.ds(r, 1)]), lane), found[c])
         for c in range(NVAR):
-            nb[g, c] = found[c]
-        return carry
-
-    lax.fori_loop(0, 4 * FACES, local, 0)
+            near[pl.ds(g * 64 + c, 8, stride=8)] = found[c]
+
+    position = lax.broadcasted_iota(jnp.int32, (LANES, LANES), 0).astype(f32).astype(bf16)
+
+    def by_matrix(g):
+        lines = [idx[pl.ds(g * 8 + a, 1)] for a in range(8)]
+        chosen = []
+        for line in lines:
+            lane = jnp.broadcast_to((line & (LANES - 1)).astype(f32).astype(bf16), (LANES, LANES))
+            one = jnp.where(position == lane, bf16(1), bf16(0))
+            chosen.append(jnp.concatenate([one, one], axis=0))
+        picked = jnp.dot(table[...], jnp.concatenate(chosen, axis=1), preferred_element_type=f32)
+        for a in range(8):
+            rows = [picked[8 * r : 8 * r + 8, LANES * a : LANES * (a + 1)] for r in range(32)]
+            near[pl.ds(pl.multiple_of((g * 8 + a) * 8, 8), 8)] = bits_select(rows, wide(lines[a] >> 7), 5)
+
+    def local(q, carry):
+        for d in range(FACES):
+            if d < 2:
+                by_lanes(q * FACES + d)
+            else:
+                by_matrix(q * FACES + d)
+        return carry
+
+    lax.fori_loop(0, 4, local, 0)
+
+    loads[3].wait()
+    loads[4].wait()
+    factors[...] = jnp.zeros_like(factors)
+    factors[0:NVAR, 0:NVAR] = left[...]
+    factors[8 : 8 + NVAR, 0:NVAR] = right[...]
+    eye = (
+        lax.broadcasted_iota(jnp.int32, (8, LANES), 0) == lax.broadcasted_iota(jnp.int32, (8, LANES), 1)
+    ).astype(f32)
+    turned = lax.dot_general(
+        eye, jnp.concatenate([factors[8:16], jnp.zeros((120, LANES), f32)], axis=0),
+        (((1,), (1,)), ((), ())), precision=lax.Precision.HIGHEST, preferred_element_type=f32,
+    )
+    lane_at = lax.broadcasted_iota(jnp.int32, (8, LANES), 1)
+    row_at = lax.broadcasted_iota(jnp.int32, (8, LANES), 0)
+    for j in range(NVAR):
+        line = factors[0:8] * wide(turned[j : j + 1])
+        line = jnp.where((lane_at == NVAR) & (row_at == j), 1.0, line)
+        high, rest = two_parts(line)
+        packed = high + pltpu.roll(high, 8, 1) + pltpu.roll(rest, 16, 1) + pltpu.roll(rest, 24, 1)
+        weights[8 * j : 8 * j + 8] = packed.astype(bf16)
+
+    loads[5].wait()
+
+    def regroup_area(k, carry):
+        q = k // 8
+        s = lax.rem(k, 8)
+        col = pl.multiple_of(k * LANES, LANES)
+        for x in range(3):
+            areas[x, pl.ds(q * 48 + s, FACES, stride=8)] = area[x, :, pl.ds(col, LANES)]
+        return carry
+
+    lax.fori_loop(0, 32, regroup_area, 0, unroll=8)
 
     rise.wait()
     sink.wait()
@@ -112,14 +195,14 @@
 
     def group(q, carry):
         first = pl.multiple_of(q * 8, 8)
-
-        def face(d, totals):
+        totals = [jnp.zeros((8, LANES), f32) for _ in range(8)]
+        for d in range(FACES):
             g = q * FACES + d
             at = pl.multiple_of(g * 8, 8)
             cells = idx[pl.ds(at, 8)]
             lane = cells & (LANES - 1)
             row = cells >> 7
-            found = [nb[g, c] for c in range(NVAR)]
+            found = [near[pl.ds(g * 64 + c, 8, stride=8)] for c in range(NVAR)]
             for r in range(8):
                 here = row == 32 + r
                 source = from_low if r < 4 else from_high
@@ -132,21 +215,24 @@
                 + mean[2] * areas[1, pl.ds(at, 8)]
                 + mean[3] * areas[2, pl.ds(at, 8)]
             )
-            largest = None
-            for i in range(NVAR):
+            for c in range(8):
+                work[d, pl.ds(c, 8, stride=8)] = mean[c] if c < NVAR else flux
+            columns = []
+            for a in range(8):
+                high, rest = two_parts(work[d, 8 * a : 8 * a + 8])
+                columns.append(jnp.concatenate([high, rest, high, rest], axis=0).astype(bf16))
+            entries = jnp.dot(weights[:, 0:32], jnp.concatenate(columns, axis=1), preferred_element_type=f32)
+            for a in range(8):
                 row_sum = None
                 for j in range(NVAR):
-                    entry = flux if i == j else None
-                    for m in range(NVAR):
-                        term = coupling[(i * NVAR + m) * NVAR + j] * mean[m]
-                        entry = term if entry is None else entry + term
-                    entry = jnp.abs(entry)
+                    entry = jnp.abs(entries[8 * j : 8 * j + 8, LANES * a : LANES * (a + 1)])
                     row_sum = entry if row_sum is None else row_sum + entry
-                largest = row_sum if largest is None else jnp.maximum(largest, row_sum)
+                work[d, 8 * a : 8 * a + 8] = row_sum
+            largest = work[d, pl.ds(0, 8, stride=8)]
+            for i in range(1, NVAR):
+                largest = jnp.maximum(largest, work[d, pl.ds(i, 8, stride=8)])
             last = flux + (largest + 0.5)
-            return tuple(t + x for t, x in zip(totals, mean + [last]))
-
-        totals = lax.fori_loop(0, FACES, face, tuple(jnp.zeros((8, LANES), jnp.float32) for _ in range(8)))
+            totals = [t + x for t, x in zip(totals, mean + [last])]
         for c in range(8):
             outbox[pl.ds(q * 64 + c, 8, stride=8)] = totals[c]
 
@@ -241,9 +327,15 @@
     sums = pl.pallas_call(
         functools.partial(sums_kernel, slabs, owners),
         out_shape=jax.ShapeDtypeStruct((8, LANES), f32),
-        in_specs=[vmem, vmem, vmem, vmem, smem, smem],
+        in_specs=[pl.BlockSpec(memory_space=pl.ANY)] * 6,
         out_specs=vmem,
         scratch_shapes=[
+            pltpu.VMEM((NVAR, 32, LANES), f32),
+            pltpu.VMEM(face_nbr.shape, jnp.int32),
+            pltpu.VMEM(halo_send.shape, jnp.int32),
+            pltpu.VMEM(face_area.shape, f32),
+            pltpu.VMEM((NVAR, NVAR), f32),
+            pltpu.VMEM((NVAR, NVAR), f32),
             pltpu.VMEM((192, LANES), jnp.int32),
             pltpu.VMEM((3, 192, LANES), f32),
             pltpu.VMEM((8, LANES), jnp.int32),
@@ -251,16 +343,21 @@
             pltpu.VMEM((28, LANES), f32),
             pltpu.VMEM((28, LANES), f32),
             pltpu.VMEM((28, LANES), f32),
-            pltpu.VMEM((24, NVAR, 8, LANES), f32),
-            pltpu.VMEM((343, 8, LANES), f32),
+            pltpu.VMEM((256, LANES), f32),
+            pltpu.VMEM((256, 2 * LANES), jnp.bfloat16),
+            pltpu.VMEM((16, LANES), f32),
+            pltpu.VMEM((56, LANES), jnp.bfloat16),
+            pltpu.VMEM((1536, LANES), f32),
+            pltpu.VMEM((FACES, 64, LANES), f32),
             pltpu.VMEM((256, LANES), f32),
             pltpu.VMEM((248, LANES), f32),
+            pltpu.SemaphoreType.DMA((6,)),
             pltpu.SemaphoreType.DMA((2,)),
             pltpu.SemaphoreType.DMA((2,)),
             pltpu.SemaphoreType.DMA,
             pltpu.SemaphoreType.DMA,
         ],
-        compiler_params=pltpu.CompilerParams(collective_id=0, has_side_effects=True),
+        compiler_params=pltpu.CompilerParams(collective_id=0, has_side_effects=True, vmem_limit_bytes=48 << 20),
         name="sums",
     )(state, face_nbr, halo_send, face_area, flux_left, flux_right)
     return pl.pallas_call(

time: 37.1 us -> 36.5 us (0.984)
  Pallas kernels: 36.9 us -> 30.7 us
  local copies, waits for them, and re-layouts: 0 us -> 5.44 us
    pallas_call x1, Pallas kernels: 34.2 us -> 28 us  [per_device(): pl.pallas_call(functools.partial(sums_kernel, slabs, owners), out_shape=j...]
    unnamed x0 -> x14, local copies, waits for them, and re-layouts: none -> 5.44 us
where the time goes in v2:
time: 36.5 us; the launch traced here: 36.2 us
  Pallas kernels  30.7 us (84%)
  local copies, waits for them, and re-layouts  5.44 us (15%)
    pallas_call x1, Pallas kernels, per_device(): pl.pallas_call(functools.partial(sums_kernel, slabs, owners), out_shape=j...  28 us
    unnamed x14, local copies, waits for them, and re-layouts  5.44 us
    pallas_call x1, Pallas kernels, per_device(): pl.pallas_call(invert_kernel, out_shape=jax.ShapeDtypeStruct((2, NVAR, NV...  2.69 us

profile of v2, /device:TPU:25, one launch (start us, length us, event | category | flops | bytes accessed | tf_op | source)
XLA Modules:
  0.0 36.2 jit_solution(16306933859017646731)
XLA Ops:
  0.0 0.0 copy-start
  0.0 1.0 %copy-done = f32[3,6,4096]{2,1,0:T(8,128)S(1)} copy-done((f32[3,6,4096]{2,1,0:T(8,128)S(1)}, f32[3,6,4096]{2,1,0:T(8,128)}, u32[]{:S(2)}) %copy-start) | copy-done | bytes 294936
  1.0 0.0 copy-start.1
  1.0 0.9 %copy-done.1 = s32[6,4096]{1,0:T(8,128)S(1)} copy-done((s32[6,4096]{1,0:T(8,128)S(1)}, s32[6,4096]{1,0:T(8,128)}, u32[]{:S(2)}) %copy-start.1) | copy-done | bytes 98328
  1.9 0.0 copy-start.2
  1.9 0.9 %copy-done.2 = f32[1,7,4096]{2,0,1:T(1,128)S(1)} copy-done((f32[1,7,4096]{2,0,1:T(1,128)S(1)}, f32[1,7,4096]{2,0,1:T(1,128)}, u32[]{:S(2)}) %copy-start.2) | copy-done | bytes 114712
  2.8 0.0 copy-start.3
  2.8 0.7 %copy-done.3 = f32[7,7]{1,0:T(8,128)S(1)} copy-done((f32[7,7]{1,0:T(8,128)S(1)}, f32[7,7]{1,0:T(8,128)}, u32[]{:S(2)}) %copy-start.3) | copy-done | bytes 220
  3.5 0.0 copy-start.4
  3.5 0.7 %copy-done.4 = f32[7,7]{1,0:T(8,128)S(1)} copy-done((f32[7,7]{1,0:T(8,128)S(1)}, f32[7,7]{1,0:T(8,128)}, u32[]{:S(2)}) %copy-start.4) | copy-done | bytes 220
  4.2 0.0 copy-start.6
  4.2 0.7 %copy-done.6 = s32[2,512]{1,0:T(2,128)S(1)} copy-done((s32[2,512]{1,0:T(2,128)S(1)}, s32[2,512]{1,0:T(2,128)}, u32[]{:S(2)}) %copy-start.6) | copy-done | bytes 4120
  4.9 28.0 %sums.1 = f32[8,128]{1,0:T(8,128)S(1)} custom-call(f32[7,32,128]{2,1,0:T(8,128)S(1)} %bitcast.2, s32[6,4096]{1,0:T(8,128)S(1)} %copy-done.1, s32[2,512]{1,0:T(2,128)S(1)} %copy-done.6, f32[3,6,4096]{2,1,0:T(8,128)S(1)} %copy-done, f32[7,7]{1,0:T(8,128)S(1)} %copy-done.3, f32[7,7]{1,0:T(8,128)S(1)} %copy-done.4), custom_call_target="tpu_custom_call" | custom-call | tf_op jit(solution)/shard_map/sums/pallas_call | solution.py:327
  32.9 0.0 copy-start.5
  32.9 0.6 %copy-done.5 = f32[8,128]{1,0:T(8,128)} copy-done((f32[8,128]{1,0:T(8,128)}, f32[8,128]{1,0:T(8,128)S(1)}, u32[]{:S(2)}) %copy-start.5) | copy-done | bytes 4120
  33.5 2.7 %invert.1 = f32[2,7,7,16,128]{4,3,2,1,0:T(8,128)} custom-call(f32[8,128]{1,0:T(8,128)} %copy-done.5, f32[1,128]{1,0:T(1,128)} %bitcast.3, f32[7,7]{1,0:T(8,128)} %left.1, f32[7,7]{1,0:T(8,128)} %right.1), custom_call_target="tpu_custom_call" | custom-call | tf_op jit(solution)/shard_map/invert/pallas_call | solution.py:363
Async XLA Ops:
  0.0 1.0 %copy-start = (f32[3,6,4096]{2,1,0:T(8,128)S(1)}, f32[3,6,4096]{2,1,0:T(8,128)}, u32[]{:S(2)}) copy-start(f32[3,6,4096]{2,1,0:T(8,128)} %area_hbm.1) | copy-start | bytes 884740
  1.0 0.9 %copy-start.1 = (s32[6,4096]{1,0:T(8,128)S(1)}, s32[6,4096]{1,0:T(8,128)}, u32[]{:S(2)}) copy-start(s32[6,4096]{1,0:T(8,128)} %nbr_hbm.1) | copy-start | bytes 294916
  1.9 0.9 %copy-start.2 = (f32[1,7,4096]{2,0,1:T(1,128)S(1)}, f32[1,7,4096]{2,0,1:T(1,128)}, u32[]{:S(2)}) copy-start(f32[1,7,4096]{2,0,1:T(1,128)} %param.7) | copy-start | bytes 344068
  2.8 0.7 %copy-start.3 = (f32[7,7]{1,0:T(8,128)S(1)}, f32[7,7]{1,0:T(8,128)}, u32[]{:S(2)}) copy-start(f32[7,7]{1,0:T(8,128)} %left.1) | copy-start | bytes 592
  3.5 0.7 %copy-start.4 = (f32[7,7]{1,0:T(8,128)S(1)}, f32[7,7]{1,0:T(8,128)}, u32[]{:S(2)}) copy-start(f32[7,7]{1,0:T(8,128)} %right.1) | copy-start | bytes 592
  4.2 0.7 %copy-start.6 = (s32[2,512]{1,0:T(2,128)S(1)}, s32[2,512]{1,0:T(2,128)}, u32[]{:S(2)}) copy-start(s32[2,512]{1,0:T(2,128)} %send_hbm.1) | copy-start | bytes 12292
  32.9 0.6 %copy-start.5 = (f32[8,128]{1,0:T(8,128)}, f32[8,128]{1,0:T(8,128)S(1)}, u32[]{:S(2)}) copy-start(f32[8,128]{1,0:T(8,128)S(1)} %sums.1) | copy-start | bytes 12292

commit v3 on v2

--- a/solution.py
+++ b/solution.py
@@ -327,7 +327,7 @@
     sums = pl.pallas_call(
         functools.partial(sums_kernel, slabs, owners),
         out_shape=jax.ShapeDtypeStruct((8, LANES), f32),
-        in_specs=[pl.BlockSpec(memory_space=pl.ANY)] * 6,
+        in_specs=[pl.BlockSpec(memory_space=pltpu.HBM)] * 6,
         out_specs=vmem,
         scratch_shapes=[
             pltpu.VMEM((NVAR, 32, LANES), f32),
@@ -357,7 +357,7 @@
             pltpu.SemaphoreType.DMA,
             pltpu.SemaphoreType.DMA,
         ],
-        compiler_params=pltpu.CompilerParams(collective_id=0, has_side_effects=True, vmem_limit_bytes=48 << 20),
+        compiler_params=pltpu.CompilerParams(collective_id=0, has_side_effects=True),
         name="sums",
     )(state, face_nbr, halo_send, face_area, flux_left, flux_right)
     return pl.pallas_call(

time: 36.5 us -> 31 us (0.85)
  local copies, waits for them, and re-layouts: 5.44 us -> 0 us
    unnamed x14 -> x0, local copies, waits for them, and re-layouts: 5.44 us -> none
where the time goes in v3:
time: 31 us; the launch traced here: 30.8 us
  Pallas kernels  30.8 us (99%)
    pallas_call x1, Pallas kernels, per_device(): pl.pallas_call(functools.partial(sums_kernel, slabs, owners), out_shape=j...  28.1 us
    pallas_call x1, Pallas kernels, per_device(): pl.pallas_call(invert_kernel, out_shape=jax.ShapeDtypeStruct((2, NVAR, NV...  2.69 us

profile of v3, /device:TPU:25, one launch (start us, length us, event | category | flops | bytes accessed | tf_op | source)
XLA Modules:
  0.0 30.8 jit_solution(13398936213302685291)
XLA Ops:
  0.0 28.1 %sums.1 = f32[8,128]{1,0:T(8,128)} custom-call(f32[7,32,128]{2,1,0:T(8,128)} %bitcast.2, s32[6,4096]{1,0:T(8,128)} %nbr_hbm.1, s32[2,512]{1,0:T(2,128)} %send_hbm.1, f32[3,6,4096]{2,1,0:T(8,128)} %area_hbm.1, f32[7,7]{1,0:T(8,128)} %left.1, f32[7,7]{1,0:T(8,128)} %right.1), custom_call_target="tpu_custom_call" | custom-call | tf_op jit(solution)/shard_map/sums/pallas_call | solution.py:327
  28.1 2.7 %invert.1 = f32[2,7,7,16,128]{4,3,2,1,0:T(8,128)} custom-call(f32[8,128]{1,0:T(8,128)} %sums.1, f32[1,128]{1,0:T(1,128)} %bitcast.3, f32[7,7]{1,0:T(8,128)} %left.1, f32[7,7]{1,0:T(8,128)} %right.1), custom_call_target="tpu_custom_call" | custom-call | tf_op jit(solution)/shard_map/invert/pallas_call | solution.py:363

commit v4 on v3

--- a/solution.py
+++ b/solution.py
@@ -31,6 +31,11 @@
     return rows[0]
 
 
+def three_parts(value):
+    high, rest = two_parts(value)
+    return high, rest, ((value - high) - rest).astype(jnp.bfloat16).astype(jnp.float32)
+
+
 def two_parts(value):
     high = value.astype(jnp.bfloat16).astype(jnp.float32)
     return high, (value - high).astype(jnp.bfloat16).astype(jnp.float32)
@@ -38,15 +43,17 @@
 
 def sums_kernel(
     slabs, owners,
-    state_hbm, nbr_hbm, send_hbm, area_hbm, left_hbm, right_hbm,
+    state_hbm, nbr_hbm, send_hbm, area_hbm, volume_hbm, left_hbm, right_hbm,
     out,
-    state, nbr, send, area, left, right,
+    state, nbr, send, area, volume, left, right,
     idx, areas, halo_idx, up, down, from_low, from_high, table_rows, table, factors, weights,
     near, work, outbox, inbox,
     in_sem, halo_send_sem, halo_recv_sem, send_sem, recv_sem,
 ):
     space = lax.axis_index("space")
     inst = lax.axis_index("inst")
+    has_above = space < slabs - 1
+    has_below = space > 0
     above = lax.rem(space + 1, slabs)
     below = lax.rem(space + slabs - 1, slabs)
     f32 = jnp.float32
@@ -55,15 +62,24 @@
     loads = [
         pltpu.make_async_copy(src, dst, in_sem.at[k])
         for k, (src, dst) in enumerate(
-            [(state_hbm, state), (send_hbm, send), (nbr_hbm, nbr), (left_hbm, left), (right_hbm, right), (area_hbm, area)]
+            [
+                (left_hbm, left), (right_hbm, right), (send_hbm, send), (state_hbm, state),
+                (nbr_hbm, nbr), (area_hbm, area), (volume_hbm, volume),
+            ]
         )
     ]
     for load in loads:
         load.start()
 
     barrier = pltpu.get_barrier_semaphore()
-    pl.semaphore_signal(barrier, inc=1, device_id={"space": above}, device_id_type=pl.DeviceIdType.MESH)
-    pl.semaphore_signal(barrier, inc=1, device_id={"space": below}, device_id_type=pl.DeviceIdType.MESH)
+
+    @pl.when(has_above)
+    def _():
+        pl.semaphore_signal(barrier, inc=1, device_id={"space": above}, device_id_type=pl.DeviceIdType.MESH)
+
+    @pl.when(has_below)
+    def _():
+        pl.semaphore_signal(barrier, inc=1, device_id={"space": below}, device_id_type=pl.DeviceIdType.MESH)
 
     def greet(step, carry):
         other = lax.rem(inst + step, owners)
@@ -72,8 +88,8 @@
 
     lax.fori_loop(1, owners, greet, 0)
 
-    loads[0].wait()
-    loads[1].wait()
+    loads[2].wait()
+    loads[3].wait()
     for k in range(4):
         halo_idx[pl.ds(k, 1)] = send[0:1, LANES * k : LANES * (k + 1)]
         halo_idx[pl.ds(4 + k, 1)] = send[1:2, LANES * k : LANES * (k + 1)]
@@ -89,7 +105,7 @@
         up[pl.ds(4 * c, 4)] = found[0:4]
         down[pl.ds(4 * c, 4)] = found[4:8]
 
-    pl.semaphore_wait(barrier, owners + 1)
+    pl.semaphore_wait(barrier, owners - 1 + has_above.astype(jnp.int32) + has_below.astype(jnp.int32))
     rise = pltpu.make_async_remote_copy(
         src_ref=up, dst_ref=from_low, send_sem=halo_send_sem.at[0], recv_sem=halo_recv_sem.at[0],
         device_id={"space": above}, device_id_type=pl.DeviceIdType.MESH,
@@ -98,65 +114,17 @@
         src_ref=down, dst_ref=from_high, send_sem=halo_send_sem.at[1], recv_sem=halo_recv_sem.at[1],
         device_id={"space": below}, device_id_type=pl.DeviceIdType.MESH,
     )
-    rise.start()
-    sink.start()
-
-    for c in range(NVAR):
-        table_rows[pl.ds(c, 32, stride=8)] = state[c]
-    table_rows[pl.ds(NVAR, 32, stride=8)] = jnp.zeros((32, LANES), f32)
-    high, rest = two_parts(table_rows[...])
-    table[:, 0:LANES] = high.astype(bf16)
-    table[:, LANES : 2 * LANES] = rest.astype(bf16)
-
-    loads[2].wait()
-
-    def regroup(k, carry):
-        q = k // 8
-        s = lax.rem(k, 8)
-        col = pl.multiple_of(k * LANES, LANES)
-        idx[pl.ds(q * 48 + s, FACES, stride=8)] = nbr[:, pl.ds(col, LANES)]
-        return carry
-
-    lax.fori_loop(0, 32, regroup, 0, unroll=8)
-
-    def by_lanes(g):
-        cells = idx[pl.ds(pl.multiple_of(g * 8, 8), 8)]
-        lane = cells & (LANES - 1)
-        row = cells >> 7
-        found = [jnp.zeros((8, LANES), f32) for _ in range(NVAR)]
-        for r in range(32):
-            here = row == r
-            for c in range(NVAR):
-                found[c] = jnp.where(here, lane_gather(wide(state[c, pl.ds(r, 1)]), lane), found[c])
-        for c in range(NVAR):
-            near[pl.ds(g * 64 + c, 8, stride=8)] = found[c]
-
-    position = lax.broadcasted_iota(jnp.int32, (LANES, LANES), 0).astype(f32).astype(bf16)
-
-    def by_matrix(g):
-        lines = [idx[pl.ds(g * 8 + a, 1)] for a in range(8)]
-        chosen = []
-        for line in lines:
-            lane = jnp.broadcast_to((line & (LANES - 1)).astype(f32).astype(bf16), (LANES, LANES))
-            one = jnp.where(position == lane, bf16(1), bf16(0))
-            chosen.append(jnp.concatenate([one, one], axis=0))
-        picked = jnp.dot(table[...], jnp.concatenate(chosen, axis=1), preferred_element_type=f32)
-        for a in range(8):
-            rows = [picked[8 * r : 8 * r + 8, LANES * a : LANES * (a + 1)] for r in range(32)]
-            near[pl.ds(pl.multiple_of((g * 8 + a) * 8, 8), 8)] = bits_select(rows, wide(lines[a] >> 7), 5)
-
-    def local(q, carry):
-        for d in range(FACES):
-            if d < 2:
-                by_lanes(q * FACES + d)
-            else:
-                by_matrix(q * FACES + d)
-        return carry
-
-    lax.fori_loop(0, 4, local, 0)
-
-    loads[3].wait()
-    loads[4].wait()
+
+    @pl.when(has_above)
+    def _():
+        rise.start()
+
+    @pl.when(has_below)
+    def _():
+        sink.start()
+
+    loads[0].wait()
+    loads[1].wait()
     factors[...] = jnp.zeros_like(factors)
     factors[0:NVAR, 0:NVAR] = left[...]
     factors[8 : 8 + NVAR, 0:NVAR] = right[...]
@@ -172,26 +140,86 @@
     for j in range(NVAR):
         line = factors[0:8] * wide(turned[j : j + 1])
         line = jnp.where((lane_at == NVAR) & (row_at == j), 1.0, line)
-        high, rest = two_parts(line)
+        high, rest, last = three_parts(line)
         packed = high + pltpu.roll(high, 8, 1) + pltpu.roll(rest, 16, 1) + pltpu.roll(rest, 24, 1)
+        packed = packed + pltpu.roll(high, 32, 1) + pltpu.roll(last, 40, 1)
         weights[8 * j : 8 * j + 8] = packed.astype(bf16)
 
-    loads[5].wait()
-
-    def regroup_area(k, carry):
+    for c in range(NVAR):
+        table_rows[pl.ds(c, 32, stride=8)] = state[c]
+    table_rows[pl.ds(NVAR, 32, stride=8)] = jnp.zeros((32, LANES), f32)
+    high, rest = two_parts(table_rows[...])
+    table[:, 0:LANES] = high.astype(bf16)
+    table[:, LANES : 2 * LANES] = rest.astype(bf16)
+
+    loads[4].wait()
+
+    def regroup(k, carry):
         q = k // 8
         s = lax.rem(k, 8)
         col = pl.multiple_of(k * LANES, LANES)
-        for x in range(3):
-            areas[x, pl.ds(q * 48 + s, FACES, stride=8)] = area[x, :, pl.ds(col, LANES)]
+        idx[pl.ds(q * 48 + s, FACES, stride=8)] = nbr[:, pl.ds(col, LANES)]
         return carry
 
-    lax.fori_loop(0, 32, regroup_area, 0, unroll=8)
-
-    rise.wait()
-    sink.wait()
-    from_low[...] = jnp.where(space > 0, from_low[...], 0.0)
-    from_high[...] = jnp.where(space < slabs - 1, from_high[...], 0.0)
+    lax.fori_loop(0, 32, regroup, 0, unroll=8)
+
+    def by_lanes(g):
+        cells = idx[pl.ds(pl.multiple_of(g * 8, 8), 8)]
+        lane = cells & (LANES - 1)
+        row = cells >> 7
+        found = [jnp.zeros((8, LANES), f32) for _ in range(NVAR)]
+        for r in range(32):
+            here = row == r
+            for c in range(NVAR):
+                found[c] = jnp.where(here, lane_gather(wide(state[c, pl.ds(r, 1)]), lane), found[c])
+        for c in range(NVAR):
+            near[pl.ds(g * 64 + c, 8, stride=8)] = found[c]
+
+    position = lax.broadcasted_iota(jnp.int32, (LANES, LANES), 0).astype(f32).astype(bf16)
+
+    def by_matrix(g):
+        lines = [idx[pl.ds(g * 8 + a, 1)] for a in range(8)]
+        chosen = []
+        for line in lines:
+            lane = jnp.broadcast_to((line & (LANES - 1)).astype(f32).astype(bf16), (LANES, LANES))
+            one = jnp.where(position == lane, bf16(1), bf16(0))
+            chosen.append(jnp.concatenate([one, one], axis=0))
+        picked = jnp.dot(table[...], jnp.concatenate(chosen, axis=1), preferred_element_type=f32)
+        for a in range(8):
+            rows = [picked[8 * r : 8 * r + 8, LANES * a : LANES * (a + 1)] for r in range(32)]
+            near[pl.ds(pl.multiple_of((g * 8 + a) * 8, 8), 8)] = bits_select(rows, wide(lines[a] >> 7), 5)
+
+    loads[5].wait()
+
+    def local(q, carry):
+        for k in range(8):
+            col = pl.multiple_of((q * 8 + k) * LANES, LANES)
+            for x in range(3):
+                areas[x, pl.ds(q * 48 + k, FACES, stride=8)] = area[x, :, pl.ds(col, LANES)]
+        for d in range(FACES):
+            if d < 2:
+                by_lanes(q * FACES + d)
+            else:
+                by_matrix(q * FACES + d)
+        return carry
+
+    lax.fori_loop(0, 4, local, 0)
+
+    @pl.when(has_below)
+    def _():
+        rise.wait_recv()
+
+    @pl.when(has_above)
+    def _():
+        sink.wait_recv()
+
+    @pl.when(space == 0)
+    def _():
+        from_low[...] = jnp.zeros_like(from_low)
+
+    @pl.when(space == slabs - 1)
+    def _():
+        from_high[...] = jnp.zeros_like(from_high)
 
     def group(q, carry):
         first = pl.multiple_of(q * 8, 8)
@@ -259,25 +287,30 @@
     total = outbox[pl.ds(pl.multiple_of(inst * 8, 8), 8)]
     for k in range(31):
         total = total + inbox[8 * k : 8 * k + 8]
-    out[...] = total
+    high, rest, last = three_parts(total)
+    parts = jnp.concatenate([high, rest, high, rest, last, high], axis=0).astype(bf16)
+    out[0:56] = jnp.dot(weights[:, 0:48], parts, preferred_element_type=f32) * (0.5 / (FACES * INSTANCES))
+    loads[6].wait()
+    out[56:64] = frequency * wide(volume[...])
     pltpu.make_async_copy(inbox, inbox, send_sem).wait()
 
-
-def invert_kernel(sums, volume, left, right, out):
-    scale = 1.0 / (2.0 * FACES * INSTANCES)
-    part = [jnp.broadcast_to(sums[pl.ds(m, 1)], (8, LANES)) for m in range(NVAR + 1)]
+    @pl.when(has_above)
+    def _():
+        rise.wait_send()
+
+    @pl.when(has_below)
+    def _():
+        sink.wait_send()
+
+
+def invert_kernel(mean, out):
     harmonic = lax.broadcasted_iota(jnp.int32, (HARM, LANES), 0).astype(jnp.float32) + 1.0
-    shift = harmonic * frequency * jnp.broadcast_to(volume[...], (HARM, LANES))
+    shift = harmonic * jnp.broadcast_to(mean[pl.ds(56, 1)], (HARM, LANES))
     real = {}
     imag = {}
     for i in range(NVAR):
         for j in range(NVAR):
-            entry = part[NVAR] if i == j else None
-            for m in range(NVAR):
-                term = (left[i, m] * right[m, j]) * part[m]
-                entry = term if entry is None else entry + term
-            entry = entry * scale
-            real[i, j] = jnp.concatenate([entry, entry], axis=0)
+            real[i, j] = jnp.broadcast_to(mean[pl.ds(8 * j + i, 1)], (HARM, LANES))
             imag[i, j] = shift if i == j else None
 
     def product(ar, ai, br, bi):
@@ -322,18 +355,18 @@
     share = cell_volume.shape[0]
     state = flow_state.reshape(NVAR, 32, LANES)
     vmem = pl.BlockSpec(memory_space=pltpu.VMEM)
-    smem = pl.BlockSpec(memory_space=pltpu.SMEM)
     f32 = jnp.float32
-    sums = pl.pallas_call(
+    mean = pl.pallas_call(
         functools.partial(sums_kernel, slabs, owners),
-        out_shape=jax.ShapeDtypeStruct((8, LANES), f32),
-        in_specs=[pl.BlockSpec(memory_space=pltpu.HBM)] * 6,
+        out_shape=jax.ShapeDtypeStruct((64, LANES), f32),
+        in_specs=[pl.BlockSpec(memory_space=pltpu.HBM)] * 7,
         out_specs=vmem,
         scratch_shapes=[
             pltpu.VMEM((NVAR, 32, LANES), f32),
             pltpu.VMEM(face_nbr.shape, jnp.int32),
             pltpu.VMEM(halo_send.shape, jnp.int32),
             pltpu.VMEM(face_area.shape, f32),
+            pltpu.VMEM((1, share), f32),
             pltpu.VMEM((NVAR, NVAR), f32),
             pltpu.VMEM((NVAR, NVAR), f32),
             pltpu.VMEM((192, LANES), jnp.int32),
@@ -351,7 +384,7 @@
             pltpu.VMEM((FACES, 64, LANES), f32),
             pltpu.VMEM((256, LANES), f32),
             pltpu.VMEM((248, LANES), f32),
-            pltpu.SemaphoreType.DMA((6,)),
+            pltpu.SemaphoreType.DMA((7,)),
             pltpu.SemaphoreType.DMA((2,)),
             pltpu.SemaphoreType.DMA((2,)),
             pltpu.SemaphoreType.DMA,
@@ -359,14 +392,14 @@
         ],
         compiler_params=pltpu.CompilerParams(collective_id=0, has_side_effects=True),
         name="sums",
-    )(state, face_nbr, halo_send, face_area, flux_left, flux_right)
+    )(state, face_nbr, halo_send, face_area, cell_volume.reshape(1, share), flux_left, flux_right)
     return pl.pallas_call(
         invert_kernel,
         out_shape=jax.ShapeDtypeStruct((2, NVAR, NVAR, HARM, share), f32),
-        in_specs=[vmem, vmem, smem, smem],
+        in_specs=[vmem],
         out_specs=vmem,
         name="invert",
-    )(sums, cell_volume.reshape(1, share), flux_left, flux_right)
+    )(mean)
 
 
 def solution(mesh):

time: 31 us -> 26.5 us (0.85)
  the two profiles are of different devices: /device:TPU:25 before, /device:TPU:31 now
where the time goes in v4:
time: 26.5 us; the launch traced here: 26.3 us
  Pallas kernels  26.3 us (99%)
    pallas_call x1, Pallas kernels, per_device(): pl.pallas_call(functools.partial(sums_kernel, slabs, owners), out_shape=j...  23.9 us
    pallas_call x1, Pallas kernels, per_device(): pl.pallas_call(invert_kernel, out_shape=jax.ShapeDtypeStruct((2, NVAR, NV...  2.34 us

profile of v4, /device:TPU:31, one launch (start us, length us, event | category | flops | bytes accessed | tf_op | source)
XLA Modules:
  0.0 26.3 jit_solution(4965013228614948305)
XLA Ops:
  0.0 23.9 %sums.1.mean = f32[64,128]{1,0:T(8,128)} custom-call(f32[7,32,128]{2,1,0:T(8,128)} %bitcast.2, s32[6,4096]{1,0:T(8,128)} %nbr_hbm.1, s32[2,512]{1,0:T(2,128)} %send_hbm.1, f32[3,6,4096]{2,1,0:T(8,128)} %area_hbm.1, f32[1,128]{1,0:T(1,128)} %bitcast.3, f32[7,7]{1,0:T(8,128)} %left_hbm.1, f32[7,7]{1,0:T(8,128)} %right_hbm.1), custom_call_target="tpu_custom_call" | custom-call | tf_op jit(solution)/shard_map/sums/pallas_call | solution.py:359
  24.0 2.3 %invert.1 = f32[2,7,7,16,128]{4,3,2,1,0:T(8,128)} custom-call(f32[64,128]{1,0:T(8,128)} %sums.1.mean), custom_call_target="tpu_custom_call" | custom-call | tf_op jit(solution)/shard_map/invert/pallas_call | solution.py:396

commit v5 on v4

--- a/solution.py
+++ b/solution.py
@@ -81,12 +81,8 @@
     def _():
         pl.semaphore_signal(barrier, inc=1, device_id={"space": below}, device_id_type=pl.DeviceIdType.MESH)
 
-    def greet(step, carry):
-        other = lax.rem(inst + step, owners)
-        pl.semaphore_signal(barrier, inc=1, device_id={"inst": other}, device_id_type=pl.DeviceIdType.MESH)
-        return carry
-
-    lax.fori_loop(1, owners, greet, 0)
+    for step in [*range(23, 15, -1), *range(31, 23, -1), *range(15, 0, -1)]:
+        pl.semaphore_signal(barrier, inc=1, device_id={"inst": inst ^ step}, device_id_type=pl.DeviceIdType.MESH)
 
     loads[2].wait()
     loads[3].wait()
@@ -221,7 +217,7 @@
     def _():
         from_high[...] = jnp.zeros_like(from_high)
 
-    def group(q, carry):
+    def group(q, own):
         first = pl.multiple_of(q * 8, 8)
         totals = [jnp.zeros((8, LANES), f32) for _ in range(8)]
         for d in range(FACES):
@@ -264,25 +260,21 @@
         for c in range(8):
             outbox[pl.ds(q * 64 + c, 8, stride=8)] = totals[c]
 
-        def post(k, carry):
-            owner = q * 8 + k
-
-            @pl.when(owner != inst)
-            def _():
-                slot = lax.rem(inst - owner + owners, owners) - 1
-                pltpu.make_async_remote_copy(
-                    src_ref=outbox.at[pl.ds(pl.multiple_of(owner * 8, 8), 8)],
-                    dst_ref=inbox.at[pl.ds(pl.multiple_of(slot * 8, 8), 8)],
-                    send_sem=send_sem, recv_sem=recv_sem,
-                    device_id={"inst": owner}, device_id_type=pl.DeviceIdType.MESH,
-                ).start()
-
-            return carry
-
-        lax.fori_loop(0, 8, post, 0)
-        return carry
-
-    lax.fori_loop(0, 4, group, 0)
+        for r in range(7, 0 if own else -1, -1):
+            owner = q * 8 + (low ^ r)
+            slot = lax.rem(inst - owner + owners, owners) - 1
+            pltpu.make_async_remote_copy(
+                src_ref=outbox.at[pl.ds(pl.multiple_of(owner * 8, 8), 8)],
+                dst_ref=inbox.at[pl.ds(pl.multiple_of(slot * 8, 8), 8)],
+                send_sem=send_sem, recv_sem=recv_sem,
+                device_id={"inst": owner}, device_id_type=pl.DeviceIdType.MESH,
+            ).start()
+
+    mine = inst // 8
+    low = lax.rem(inst, 8)
+    for away in (2, 1, 3):
+        group(lax.rem(mine + away, 4), False)
+    group(mine, True)
     pltpu.make_async_copy(inbox, inbox, recv_sem).wait()
     total = outbox[pl.ds(pl.multiple_of(inst * 8, 8), 8)]
     for k in range(31):
@@ -390,14 +382,18 @@
             pltpu.SemaphoreType.DMA,
             pltpu.SemaphoreType.DMA,
         ],
-        compiler_params=pltpu.CompilerParams(collective_id=0, has_side_effects=True),
+        compiler_params=pltpu.CompilerParams(collective_id=0, has_side_effects=True, vmem_limit_bytes=24 << 20),
         name="sums",
-    )(state, face_nbr, halo_send, face_area, cell_volume.reshape(1, share), flux_left, flux_right)
+    )(*[
+        pltpu.with_memory_space_constraint(x, pltpu.HBM)
+        for x in (state, face_nbr, halo_send, face_area, cell_volume.reshape(1, share), flux_left, flux_right)
+    ])
     return pl.pallas_call(
         invert_kernel,
         out_shape=jax.ShapeDtypeStruct((2, NVAR, NVAR, HARM, share), f32),
         in_specs=[vmem],
         out_specs=vmem,
+        compiler_params=pltpu.CompilerParams(vmem_limit_bytes=8 << 20),
         name="invert",
     )(mean)
 

time: 26.5 us -> 24.7 us (0.932)
  the two profiles are of different devices: /device:TPU:31 before, /device:TPU:7 now
where the time goes in v5:
time: 24.7 us; the launch traced here: 24.6 us
  Pallas kernels  24.6 us (100%)
    pallas_call x1, Pallas kernels, per_device(): pl.pallas_call(functools.partial(sums_kernel, slabs, owners), out_shape=j...  23 us
    pallas_call x1, Pallas kernels, per_device(): pl.pallas_call(invert_kernel, out_shape=jax.ShapeDtypeStruct((2, NVAR, NV...  1.58 us

profile of v5, /device:TPU:7, one launch (start us, length us, event | category | flops | bytes accessed | tf_op | source)
XLA Modules:
  0.0 24.6 jit_solution(13188182594268590591)
XLA Ops:
  0.0 23.0 %sums.1.mean = f32[64,128]{1,0:T(8,128)S(1)} custom-call(f32[7,32,128]{2,1,0:T(8,128)} %bitcast.2, s32[6,4096]{1,0:T(8,128)} %nbr_hbm.1, s32[2,512]{1,0:T(2,128)} %send_hbm.1, f32[3,6,4096]{2,1,0:T(8,128)} %area_hbm.1, f32[1,128]{1,0:T(1,128)} %bitcast.3, f32[7,7]{1,0:T(8,128)} %left_hbm.1, f32[7,7]{1,0:T(8,128)} %right_hbm.1), custom_call_target="tpu_custom_call" | custom-call | tf_op jit(solution)/shard_map/sums/pallas_call | solution.py:351
  23.0 1.6 %invert.1 = f32[2,7,7,16,128]{4,3,2,1,0:T(8,128)} custom-call(f32[64,128]{1,0:T(8,128)S(1)} %sums.1.mean), custom_call_target="tpu_custom_call" | custom-call | tf_op jit(solution)/shard_map/invert/pallas_call | solution.py:391

commit v6 on v5

--- a/solution.py
+++ b/solution.py
@@ -48,7 +48,7 @@
     state, nbr, send, area, volume, left, right,
     idx, areas, halo_idx, up, down, from_low, from_high, table_rows, table, factors, weights,
     near, work, outbox, inbox,
-    in_sem, halo_send_sem, halo_recv_sem, send_sem, recv_sem,
+    in_sem, halo_send_sem, halo_recv_sem, send_sem, recv_sem, round_sem,
 ):
     space = lax.axis_index("space")
     inst = lax.axis_index("inst")
@@ -63,7 +63,7 @@
         pltpu.make_async_copy(src, dst, in_sem.at[k])
         for k, (src, dst) in enumerate(
             [
-                (left_hbm, left), (right_hbm, right), (send_hbm, send), (state_hbm, state),
+                (send_hbm, send), (state_hbm, state), (left_hbm, left), (right_hbm, right),
                 (nbr_hbm, nbr), (area_hbm, area), (volume_hbm, volume),
             ]
         )
@@ -81,11 +81,11 @@
     def _():
         pl.semaphore_signal(barrier, inc=1, device_id={"space": below}, device_id_type=pl.DeviceIdType.MESH)
 
-    for step in [*range(23, 15, -1), *range(31, 23, -1), *range(15, 0, -1)]:
-        pl.semaphore_signal(barrier, inc=1, device_id={"inst": inst ^ step}, device_id_type=pl.DeviceIdType.MESH)
-
-    loads[2].wait()
-    loads[3].wait()
+    for partner in (16, 6, 7, 4, 5, 8, 24, 2, 3, 1):
+        pl.semaphore_signal(barrier, inc=1, device_id={"inst": inst ^ partner}, device_id_type=pl.DeviceIdType.MESH)
+
+    loads[0].wait()
+    loads[1].wait()
     for k in range(4):
         halo_idx[pl.ds(k, 1)] = send[0:1, LANES * k : LANES * (k + 1)]
         halo_idx[pl.ds(4 + k, 1)] = send[1:2, LANES * k : LANES * (k + 1)]
@@ -101,63 +101,47 @@
         up[pl.ds(4 * c, 4)] = found[0:4]
         down[pl.ds(4 * c, 4)] = found[4:8]
 
-    pl.semaphore_wait(barrier, owners - 1 + has_above.astype(jnp.int32) + has_below.astype(jnp.int32))
-    rise = pltpu.make_async_remote_copy(
-        src_ref=up, dst_ref=from_low, send_sem=halo_send_sem.at[0], recv_sem=halo_recv_sem.at[0],
-        device_id={"space": above}, device_id_type=pl.DeviceIdType.MESH,
-    )
-    sink = pltpu.make_async_remote_copy(
-        src_ref=down, dst_ref=from_high, send_sem=halo_send_sem.at[1], recv_sem=halo_recv_sem.at[1],
-        device_id={"space": below}, device_id_type=pl.DeviceIdType.MESH,
-    )
-
-    @pl.when(has_above)
-    def _():
-        rise.start()
-
-    @pl.when(has_below)
-    def _():
-        sink.start()
-
-    loads[0].wait()
-    loads[1].wait()
-    factors[...] = jnp.zeros_like(factors)
-    factors[0:NVAR, 0:NVAR] = left[...]
-    factors[8 : 8 + NVAR, 0:NVAR] = right[...]
-    eye = (
-        lax.broadcasted_iota(jnp.int32, (8, LANES), 0) == lax.broadcasted_iota(jnp.int32, (8, LANES), 1)
-    ).astype(f32)
-    turned = lax.dot_general(
-        eye, jnp.concatenate([factors[8:16], jnp.zeros((120, LANES), f32)], axis=0),
-        (((1,), (1,)), ((), ())), precision=lax.Precision.HIGHEST, preferred_element_type=f32,
-    )
-    lane_at = lax.broadcasted_iota(jnp.int32, (8, LANES), 1)
-    row_at = lax.broadcasted_iota(jnp.int32, (8, LANES), 0)
-    for j in range(NVAR):
-        line = factors[0:8] * wide(turned[j : j + 1])
-        line = jnp.where((lane_at == NVAR) & (row_at == j), 1.0, line)
-        high, rest, last = three_parts(line)
-        packed = high + pltpu.roll(high, 8, 1) + pltpu.roll(rest, 16, 1) + pltpu.roll(rest, 24, 1)
-        packed = packed + pltpu.roll(high, 32, 1) + pltpu.roll(last, 40, 1)
-        weights[8 * j : 8 * j + 8] = packed.astype(bf16)
-
-    for c in range(NVAR):
-        table_rows[pl.ds(c, 32, stride=8)] = state[c]
-    table_rows[pl.ds(NVAR, 32, stride=8)] = jnp.zeros((32, LANES), f32)
-    high, rest = two_parts(table_rows[...])
-    table[:, 0:LANES] = high.astype(bf16)
-    table[:, LANES : 2 * LANES] = rest.astype(bf16)
-
-    loads[4].wait()
-
-    def regroup(k, carry):
-        q = k // 8
-        s = lax.rem(k, 8)
-        col = pl.multiple_of(k * LANES, LANES)
-        idx[pl.ds(q * 48 + s, FACES, stride=8)] = nbr[:, pl.ds(col, LANES)]
-        return carry
-
-    lax.fori_loop(0, 32, regroup, 0, unroll=8)
+    def prepare():
+        loads[5].wait()
+        loads[2].wait()
+        loads[3].wait()
+        factors[...] = jnp.zeros_like(factors)
+        factors[0:NVAR, 0:NVAR] = left[...]
+        factors[8 : 8 + NVAR, 0:NVAR] = right[...]
+        eye = (
+            lax.broadcasted_iota(jnp.int32, (8, LANES), 0) == lax.broadcasted_iota(jnp.int32, (8, LANES), 1)
+        ).astype(f32)
+        turned = lax.dot_general(
+            eye, jnp.concatenate([factors[8:16], jnp.zeros((120, LANES), f32)], axis=0),
+            (((1,), (1,)), ((), ())), precision=lax.Precision.HIGHEST, preferred_element_type=f32,
+        )
+        lane_at = lax.broadcasted_iota(jnp.int32, (8, LANES), 1)
+        row_at = lax.broadcasted_iota(jnp.int32, (8, LANES), 0)
+        for j in range(NVAR):
+            line = factors[0:8] * wide(turned[j : j + 1])
+            line = jnp.where((lane_at == NVAR) & (row_at == j), 1.0, line)
+            high, rest, last = three_parts(line)
+            packed = high + pltpu.roll(high, 8, 1) + pltpu.roll(rest, 16, 1) + pltpu.roll(rest, 24, 1)
+            packed = packed + pltpu.roll(high, 32, 1) + pltpu.roll(last, 40, 1)
+            weights[8 * j : 8 * j + 8] = packed.astype(bf16)
+
+        for c in range(NVAR):
+            table_rows[pl.ds(c, 32, stride=8)] = state[c]
+        table_rows[pl.ds(NVAR, 32, stride=8)] = jnp.zeros((32, LANES), f32)
+        high, rest = two_parts(table_rows[...])
+        table[:, 0:LANES] = high.astype(bf16)
+        table[:, LANES : 2 * LANES] = rest.astype(bf16)
+
+        loads[4].wait()
+
+        def regroup(k, carry):
+            q = k // 8
+            s = lax.rem(k, 8)
+            col = pl.multiple_of(k * LANES, LANES)
+            idx[pl.ds(q * 48 + s, FACES, stride=8)] = nbr[:, pl.ds(col, LANES)]
+            return carry
+
+        lax.fori_loop(0, 32, regroup, 0, unroll=8)
 
     def by_lanes(g):
         cells = idx[pl.ds(pl.multiple_of(g * 8, 8), 8)]
@@ -185,24 +169,46 @@
             rows = [picked[8 * r : 8 * r + 8, LANES * a : LANES * (a + 1)] for r in range(32)]
             near[pl.ds(pl.multiple_of((g * 8 + a) * 8, 8), 8)] = bits_select(rows, wide(lines[a] >> 7), 5)
 
-    loads[5].wait()
-
-    def local(q, carry):
-        for k in range(8):
-            col = pl.multiple_of((q * 8 + k) * LANES, LANES)
+    def local(h, carry):
+        for k in range(16):
+            q = h * 2 + k // 8
+            col = pl.multiple_of((h * 16 + k) * LANES, LANES)
             for x in range(3):
-                areas[x, pl.ds(q * 48 + k, FACES, stride=8)] = area[x, :, pl.ds(col, LANES)]
-        for d in range(FACES):
-            if d < 2:
-                by_lanes(q * FACES + d)
+                areas[x, pl.ds(q * 48 + k % 8, FACES, stride=8)] = area[x, :, pl.ds(col, LANES)]
+        for d in range(2 * FACES):
+            if d in (0, 2, 5, 7, 10):
+                by_lanes(h * 2 * FACES + d)
             else:
-                by_matrix(q * FACES + d)
+                by_matrix(h * 2 * FACES + d)
         return carry
 
-    lax.fori_loop(0, 4, local, 0)
+    pl.semaphore_wait(barrier, 10 + has_above.astype(jnp.int32) + has_below.astype(jnp.int32))
+    rise = pltpu.make_async_remote_copy(
+        src_ref=up, dst_ref=from_low, send_sem=halo_send_sem.at[0], recv_sem=halo_recv_sem.at[0],
+        device_id={"space": above}, device_id_type=pl.DeviceIdType.MESH,
+    )
+    sink = pltpu.make_async_remote_copy(
+        src_ref=down, dst_ref=from_high, send_sem=halo_send_sem.at[1], recv_sem=halo_recv_sem.at[1],
+        device_id={"space": below}, device_id_type=pl.DeviceIdType.MESH,
+    )
+
+    @pl.when(has_above)
+    def _():
+        rise.start()
 
     @pl.when(has_below)
     def _():
+        sink.start()
+
+    for partner in (16, 8, 24):
+        pl.semaphore_signal(round_sem, inc=1, device_id={"inst": inst ^ partner}, device_id_type=pl.DeviceIdType.MESH)
+
+    prepare()
+    lax.fori_loop(0, 2, local, 0)
+
+
+    @pl.when(has_below)
+    def _():
         rise.wait_recv()
 
     @pl.when(has_above)
@@ -217,7 +223,7 @@
     def _():
         from_high[...] = jnp.zeros_like(from_high)
 
-    def group(q, own):
+    def group(q, opening, own):
         first = pl.multiple_of(q * 8, 8)
         totals = [jnp.zeros((8, LANES), f32) for _ in range(8)]
         for d in range(FACES):
@@ -260,6 +266,8 @@
         for c in range(8):
             outbox[pl.ds(q * 64 + c, 8, stride=8)] = totals[c]
 
+        if opening:
+            pl.semaphore_wait(round_sem, 3)
         for r in range(7, 0 if own else -1, -1):
             owner = q * 8 + (low ^ r)
             slot = lax.rem(inst - owner + owners, owners) - 1
@@ -273,8 +281,8 @@
     mine = inst // 8
     low = lax.rem(inst, 8)
     for away in (2, 1, 3):
-        group(lax.rem(mine + away, 4), False)
-    group(mine, True)
+        group(lax.rem(mine + away, 4), away == 2, False)
+    group(mine, False, True)
     pltpu.make_async_copy(inbox, inbox, recv_sem).wait()
     total = outbox[pl.ds(pl.multiple_of(inst * 8, 8), 8)]
     for k in range(31):
@@ -381,6 +389,7 @@
             pltpu.SemaphoreType.DMA((2,)),
             pltpu.SemaphoreType.DMA,
             pltpu.SemaphoreType.DMA,
+            pltpu.SemaphoreType.REGULAR,
         ],
         compiler_params=pltpu.CompilerParams(collective_id=0, has_side_effects=True, vmem_limit_bytes=24 << 20),
         name="sums",

time: 24.7 us -> 24.1 us (0.976)
  Pallas kernels: 24.6 us -> 23.9 us
    pallas_call x1, Pallas kernels: 23 us -> 22.3 us  [per_device(): pl.pallas_call(functools.partial(sums_kernel, slabs, owners), out_shape=j...]
where the time goes in v6:
time: 24.1 us; the launch traced here: 23.9 us
  Pallas kernels  23.9 us (99%)
    pallas_call x1, Pallas kernels, per_device(): pl.pallas_call(functools.partial(sums_kernel, slabs, owners), out_shape=j...  22.3 us
    pallas_call x1, Pallas kernels, per_device(): pl.pallas_call(invert_kernel, out_shape=jax.ShapeDtypeStruct((2, NVAR, NV...  1.58 us

profile of v6, /device:TPU:7, one launch (start us, length us, event | category | flops | bytes accessed | tf_op | source)
XLA Modules:
  0.0 23.9 jit_solution(16955672802129705558)
XLA Ops:
  0.0 22.3 %sums.1.mean = f32[64,128]{1,0:T(8,128)S(1)} custom-call(f32[7,32,128]{2,1,0:T(8,128)} %bitcast.2, s32[6,4096]{1,0:T(8,128)} %nbr_hbm.1, s32[2,512]{1,0:T(2,128)} %send_hbm.1, f32[3,6,4096]{2,1,0:T(8,128)} %area_hbm.1, f32[1,128]{1,0:T(1,128)} %bitcast.3, f32[7,7]{1,0:T(8,128)} %left_hbm.1, f32[7,7]{1,0:T(8,128)} %right_hbm.1), custom_call_target="tpu_custom_call" | custom-call | tf_op jit(solution)/shard_map/sums/pallas_call | solution.py:359
  22.4 1.6 %invert.1 = f32[2,7,7,16,128]{4,3,2,1,0:T(8,128)} custom-call(f32[64,128]{1,0:T(8,128)S(1)} %sums.1.mean), custom_call_target="tpu_custom_call" | custom-call | tf_op jit(solution)/shard_map/invert/pallas_call | solution.py:400

commit v7 on v6

--- a/solution.py
+++ b/solution.py
@@ -41,13 +41,17 @@
     return high, (value - high).astype(jnp.bfloat16).astype(jnp.float32)
 
 
+def relative(p):
+    return (p & 16) | ((p & 8) >> 1) | ((p & 4) << 1) | (p & 3)
+
+
 def sums_kernel(
     slabs, owners,
     state_hbm, nbr_hbm, send_hbm, area_hbm, volume_hbm, left_hbm, right_hbm,
     out,
     state, nbr, send, area, volume, left, right,
     idx, areas, halo_idx, up, down, from_low, from_high, table_rows, table, factors, weights,
-    near, work, outbox, inbox,
+    own, near, work, outbox, inbox,
     in_sem, halo_send_sem, halo_recv_sem, send_sem, recv_sem, round_sem,
 ):
     space = lax.axis_index("space")
@@ -134,14 +138,15 @@
 
         loads[4].wait()
 
-        def regroup(k, carry):
-            q = k // 8
-            s = lax.rem(k, 8)
-            col = pl.multiple_of(k * LANES, LANES)
-            idx[pl.ds(q * 48 + s, FACES, stride=8)] = nbr[:, pl.ds(col, LANES)]
-            return carry
-
-        lax.fori_loop(0, 32, regroup, 0, unroll=8)
+        for p in range(32):
+            q, k = p // 8, p % 8
+            block = inst ^ relative(p)
+            col = pl.multiple_of(block * LANES, LANES)
+            idx[pl.ds(q * 48 + k, FACES, stride=8)] = nbr[:, pl.ds(col, LANES)]
+            for x in range(3):
+                areas[x, pl.ds(q * 48 + k, FACES, stride=8)] = area[x, :, pl.ds(col, LANES)]
+            for c in range(NVAR):
+                own[c, pl.ds(p, 1)] = state[c, pl.ds(block, 1)]
 
     def by_lanes(g):
         cells = idx[pl.ds(pl.multiple_of(g * 8, 8), 8)]
@@ -170,11 +175,6 @@
             near[pl.ds(pl.multiple_of((g * 8 + a) * 8, 8), 8)] = bits_select(rows, wide(lines[a] >> 7), 5)
 
     def local(h, carry):
-        for k in range(16):
-            q = h * 2 + k // 8
-            col = pl.multiple_of((h * 16 + k) * LANES, LANES)
-            for x in range(3):
-                areas[x, pl.ds(q * 48 + k % 8, FACES, stride=8)] = area[x, :, pl.ds(col, LANES)]
         for d in range(2 * FACES):
             if d in (0, 2, 5, 7, 10):
                 by_lanes(h * 2 * FACES + d)
@@ -223,12 +223,12 @@
     def _():
         from_high[...] = jnp.zeros_like(from_high)
 
-    def group(q, opening, own):
-        first = pl.multiple_of(q * 8, 8)
+    def group(q, opening):
+        first = q * 8
         totals = [jnp.zeros((8, LANES), f32) for _ in range(8)]
         for d in range(FACES):
             g = q * FACES + d
-            at = pl.multiple_of(g * 8, 8)
+            at = g * 8
             cells = idx[pl.ds(at, 8)]
             lane = cells & (LANES - 1)
             row = cells >> 7
@@ -239,7 +239,7 @@
                 for c in range(NVAR):
                     line = source[pl.ds(4 * c + r % 4, 1)]
                     found[c] = jnp.where(here, lane_gather(wide(line), lane), found[c])
-            mean = [0.5 * (state[c, pl.ds(first, 8)] + found[c]) for c in range(NVAR)]
+            mean = [0.5 * (own[c, first : first + 8] + found[c]) for c in range(NVAR)]
             flux = (
                 mean[1] * areas[0, pl.ds(at, 8)]
                 + mean[2] * areas[1, pl.ds(at, 8)]
@@ -268,23 +268,18 @@
 
         if opening:
             pl.semaphore_wait(round_sem, 3)
-        for r in range(7, 0 if own else -1, -1):
-            owner = q * 8 + (low ^ r)
-            slot = lax.rem(inst - owner + owners, owners) - 1
+        for p in range(first + 7, max(first, 1) - 1, -1):
+            rel = relative(p)
             pltpu.make_async_remote_copy(
-                src_ref=outbox.at[pl.ds(pl.multiple_of(owner * 8, 8), 8)],
-                dst_ref=inbox.at[pl.ds(pl.multiple_of(slot * 8, 8), 8)],
+                src_ref=outbox.at[pl.ds(8 * p, 8)], dst_ref=inbox.at[pl.ds(8 * (rel - 1), 8)],
                 send_sem=send_sem, recv_sem=recv_sem,
-                device_id={"inst": owner}, device_id_type=pl.DeviceIdType.MESH,
+                device_id={"inst": inst ^ rel}, device_id_type=pl.DeviceIdType.MESH,
             ).start()
 
-    mine = inst // 8
-    low = lax.rem(inst, 8)
-    for away in (2, 1, 3):
-        group(lax.rem(mine + away, 4), away == 2, False)
-    group(mine, False, True)
+    for q in (3, 2, 1, 0):
+        group(q, q == 3)
     pltpu.make_async_copy(inbox, inbox, recv_sem).wait()
-    total = outbox[pl.ds(pl.multiple_of(inst * 8, 8), 8)]
+    total = outbox[0:8]
     for k in range(31):
         total = total + inbox[8 * k : 8 * k + 8]
     high, rest, last = three_parts(total)
@@ -380,6 +375,7 @@
             pltpu.VMEM((256, 2 * LANES), jnp.bfloat16),
             pltpu.VMEM((16, LANES), f32),
             pltpu.VMEM((56, LANES), jnp.bfloat16),
+            pltpu.VMEM((NVAR, 32, LANES), f32),
             pltpu.VMEM((1536, LANES), f32),
             pltpu.VMEM((FACES, 64, LANES), f32),
             pltpu.VMEM((256, LANES), f32),

time: 24.1 us -> 23.7 us (0.983)
  Pallas kernels: 23.9 us -> 23.6 us
    pallas_call x1, Pallas kernels: 22.3 us -> 22 us  [per_device(): pl.pallas_call(functools.partial(sums_kernel, slabs, owners), out_shape=j...]
where the time goes in v7:
time: 23.7 us; the launch traced here: 23.6 us
  Pallas kernels  23.6 us (100%)
    pallas_call x1, Pallas kernels, per_device(): pl.pallas_call(functools.partial(sums_kernel, slabs, owners), out_shape=j...  22 us
    pallas_call x1, Pallas kernels, per_device(): pl.pallas_call(invert_kernel, out_shape=jax.ShapeDtypeStruct((2, NVAR, NV...  1.58 us

profile of v7, /device:TPU:7, one launch (start us, length us, event | category | flops | bytes accessed | tf_op | source)
XLA Modules:
  0.0 23.6 jit_solution(16121284035054899204)
XLA Ops:
  0.0 22.0 %sums.1.mean = f32[64,128]{1,0:T(8,128)S(1)} custom-call(f32[7,32,128]{2,1,0:T(8,128)} %bitcast.2, s32[6,4096]{1,0:T(8,128)} %nbr_hbm.1, s32[2,512]{1,0:T(2,128)} %send_hbm.1, f32[3,6,4096]{2,1,0:T(8,128)} %area_hbm.1, f32[1,128]{1,0:T(1,128)} %bitcast.3, f32[7,7]{1,0:T(8,128)} %left_hbm.1, f32[7,7]{1,0:T(8,128)} %right_hbm.1), custom_call_target="tpu_custom_call" | custom-call | tf_op jit(solution)/shard_map/sums/pallas_call | solution.py:354
  22.0 1.6 %invert.1 = f32[2,7,7,16,128]{4,3,2,1,0:T(8,128)} custom-call(f32[64,128]{1,0:T(8,128)S(1)} %sums.1.mean), custom_call_target="tpu_custom_call" | custom-call | tf_op jit(solution)/shard_map/invert/pallas_call | solution.py:396

commit v8 on v7

--- a/solution.py
+++ b/solution.py
@@ -298,14 +298,14 @@
         sink.wait_send()
 
 
-def invert_kernel(mean, out):
-    harmonic = lax.broadcasted_iota(jnp.int32, (HARM, LANES), 0).astype(jnp.float32) + 1.0
-    shift = harmonic * jnp.broadcast_to(mean[pl.ds(56, 1)], (HARM, LANES))
+def invert_half(mean, half, ready):
+    harmonic = lax.broadcasted_iota(jnp.int32, (8, LANES), 0).astype(jnp.float32) + (8.0 * half + 1.0)
+    shift = harmonic * jnp.broadcast_to(mean[pl.ds(56, 1)], (8, LANES))
     real = {}
     imag = {}
     for i in range(NVAR):
         for j in range(NVAR):
-            real[i, j] = jnp.broadcast_to(mean[pl.ds(8 * j + i, 1)], (HARM, LANES))
+            real[i, j] = jnp.broadcast_to(mean[pl.ds(8 * j + i, 1)], (8, LANES))
             imag[i, j] = shift if i == j else None
 
     def product(ar, ai, br, bi):
@@ -340,8 +340,19 @@
             real[i, k], imag[i, k] = -xr, -xi
     for i in range(NVAR):
         for j in range(NVAR):
-            out[0, i, j] = real[i, j]
-            out[1, i, j] = imag[i, j]
+            ready[half, 0, i, j] = real[i, j]
+            ready[half, 1, i, j] = imag[i, j]
+
+
+def invert_kernel(mean, out, ready, sem):
+    copies = []
+    for half in range(2):
+        invert_half(mean, half, ready)
+        copy = pltpu.make_async_copy(ready.at[half], out.at[:, :, :, pl.ds(8 * half, 8)], sem.at[half])
+        copy.start()
+        copies.append(copy)
+    for copy in copies:
+        copy.wait()
 
 
 def per_device(flow_state, face_nbr, halo_send, face_area, cell_volume, flux_left, flux_right):
@@ -397,7 +408,8 @@
         invert_kernel,
         out_shape=jax.ShapeDtypeStruct((2, NVAR, NVAR, HARM, share), f32),
         in_specs=[vmem],
-        out_specs=vmem,
+        out_specs=pl.BlockSpec(memory_space=pltpu.HBM),
+        scratch_shapes=[pltpu.VMEM((2, 2, NVAR, NVAR, 8, share), f32), pltpu.SemaphoreType.DMA((2,))],
         compiler_params=pltpu.CompilerParams(vmem_limit_bytes=8 << 20),
         name="invert",
     )(mean)

time: 23.7 us -> 23.6 us (level)
  no operation moved by 1% of the time
where the time goes in v8:
time: 23.6 us; the launch traced here: 23.5 us
  Pallas kernels  23.5 us (100%)
    pallas_call x1, Pallas kernels, per_device(): pl.pallas_call(functools.partial(sums_kernel, slabs, owners), out_shape=j...  22 us
    pallas_call x1, Pallas kernels, per_device(): pl.pallas_call(invert_kernel, out_shape=jax.ShapeDtypeStruct((2, NVAR, NV...  1.48 us

profile of v8, /device:TPU:7, one launch (start us, length us, event | category | flops | bytes accessed | tf_op | source)
XLA Modules:
  0.0 23.5 jit_solution(6360904200954353156)
XLA Ops:
  0.0 22.0 %sums.1.mean = f32[64,128]{1,0:T(8,128)S(1)} custom-call(f32[7,32,128]{2,1,0:T(8,128)} %bitcast.2, s32[6,4096]{1,0:T(8,128)} %nbr_hbm.1, s32[2,512]{1,0:T(2,128)} %send_hbm.1, f32[3,6,4096]{2,1,0:T(8,128)} %area_hbm.1, f32[1,128]{1,0:T(1,128)} %bitcast.3, f32[7,7]{1,0:T(8,128)} %left_hbm.1, f32[7,7]{1,0:T(8,128)} %right_hbm.1), custom_call_target="tpu_custom_call" | custom-call | tf_op jit(solution)/shard_map/sums/pallas_call | solution.py:365
  22.0 1.5 %invert.1 = f32[2,7,7,16,128]{4,3,2,1,0:T(8,128)} custom-call(f32[64,128]{1,0:T(8,128)S(1)} %sums.1.mean), custom_call_target="tpu_custom_call" | custom-call | tf_op jit(solution)/shard_map/invert/pallas_call | solution.py:407

commit v9 on v8

--- a/solution.py
+++ b/solution.py
@@ -278,15 +278,16 @@
 
     for q in (3, 2, 1, 0):
         group(q, q == 3)
+    loads[6].wait()
+    out[56:64] = frequency * wide(volume[...])
     pltpu.make_async_copy(inbox, inbox, recv_sem).wait()
-    total = outbox[0:8]
-    for k in range(31):
-        total = total + inbox[8 * k : 8 * k + 8]
+    terms = [outbox[0:8]] + [inbox[8 * k : 8 * k + 8] for k in range(31)]
+    while len(terms) > 1:
+        terms = [a + b for a, b in zip(terms[::2], terms[1::2])]
+    total = terms[0]
     high, rest, last = three_parts(total)
     parts = jnp.concatenate([high, rest, high, rest, last, high], axis=0).astype(bf16)
     out[0:56] = jnp.dot(weights[:, 0:48], parts, preferred_element_type=f32) * (0.5 / (FACES * INSTANCES))
-    loads[6].wait()
-    out[56:64] = frequency * wide(volume[...])
     pltpu.make_async_copy(inbox, inbox, send_sem).wait()
 
     @pl.when(has_above)

time: 23.6 us -> 23.6 us (level)
  no operation moved by 1% of the time
where the time goes in v9:
time: 23.6 us; the launch traced here: 23.4 us
  Pallas kernels  23.4 us (99%)
    pallas_call x1, Pallas kernels, per_device(): pl.pallas_call(functools.partial(sums_kernel, slabs, owners), out_shape=j...  21.9 us
    pallas_call x1, Pallas kernels, per_device(): pl.pallas_call(invert_kernel, out_shape=jax.ShapeDtypeStruct((2, NVAR, NV...  1.48 us

profile of v9, /device:TPU:7, one launch (start us, length us, event | category | flops | bytes accessed | tf_op | source)
XLA Modules:
  0.0 23.4 jit_solution(5390135921458308873)
XLA Ops:
  0.0 21.9 %sums.1.mean = f32[64,128]{1,0:T(8,128)S(1)} custom-call(f32[7,32,128]{2,1,0:T(8,128)} %bitcast.2, s32[6,4096]{1,0:T(8,128)} %nbr_hbm.1, s32[2,512]{1,0:T(2,128)} %send_hbm.1, f32[3,6,4096]{2,1,0:T(8,128)} %area_hbm.1, f32[1,128]{1,0:T(1,128)} %bitcast.3, f32[7,7]{1,0:T(8,128)} %left_hbm.1, f32[7,7]{1,0:T(8,128)} %right_hbm.1), custom_call_target="tpu_custom_call" | custom-call | tf_op jit(solution)/shard_map/sums/pallas_call | solution.py:366
  22.0 1.5 %invert.1 = f32[2,7,7,16,128]{4,3,2,1,0:T(8,128)} custom-call(f32[64,128]{1,0:T(8,128)S(1)} %sums.1.mean), custom_call_target="tpu_custom_call" | custom-call | tf_op jit(solution)/shard_map/invert/pallas_call | solution.py:408
